TPU v7x, 128 devices: a whole 4x4x4 slice. The times are simulated.
128 devices in a mesh: seq: 32 (over y, x, core), chan: 4 (over z).
Axes of the slice: x: 4, y: 4, z: 4, core: 2. Of those that a mesh axis runs over, the one named last changes fastest.
Arguments:
- doc_ids: int32 [8192], replicated, may hold values from 0 to 15, never falling along the last dimension, each value on 1 to 1024 neighbouring positions
- attn_queries: bfloat16 [8192, 8192], P(('seq', 'chan')), may hold values from -6 to 6
- attn_keys: bfloat16 [8192, 8192], P(('seq', 'chan')), may hold values from -6 to 6
- attn_values: bfloat16 [8192, 8192], P(('seq', 'chan')), may hold values from -6 to 6
- attn_cot: bfloat16 [8192, 8192], P(('seq', 'chan')), may hold values from -6 to 6
Outputs:
- attn_out: bfloat16 [8192, 8192], P('seq', 'chan')
- query_grad: bfloat16 [8192, 8192], P('seq', 'chan')
- key_grad: bfloat16 [8192, 8192], P('seq', 'chan')
- value_grad: bfloat16 [8192, 8192], P('seq', 'chan')
Inputs may be any that keep to these rules, and one draw needn't show every extreme that they name: `doc_ids`: documents are runs of equal ids that never fall; each holds 1 to 1024 tokens and one holds exactly 1024.
All inputs are finite; a program needn't handle non-finite values.
Results may differ from a plain program's by a relative error of at most 0.03.
Values may be sent and summed in bfloat16 or wider, within the bound.
A program may use at most 256 MiB of HBM per device.

v0:
```python
from functools import reduce

import jax
import jax.numpy as jnp
from jax import lax
from jax.sharding import PartitionSpec as P

HEAD_DIM = 128
SPAN_SH = 4


NEG = -1e30


def shifted(value, axis, by):
    count = lax.axis_size(axis)
    pairs = [(i, i + by) for i in range(count) if 0 <= i + by < count]
    return lax.ppermute(value, axis, pairs)


def guarded(work, operands):
    return work(*operands)


def allowed_pairs(doc_ids, query_shard, key_shard, row_count, shard_total):
    offsets = jnp.arange(row_count, dtype=jnp.int32)
    query_pos = query_shard * row_count + offsets
    key_pos = key_shard * row_count + offsets
    query_doc = lax.dynamic_slice_in_dim(doc_ids, query_shard * row_count, row_count)
    key_doc = lax.dynamic_slice_in_dim(doc_ids, key_shard * row_count, row_count)
    inside = (key_shard >= 0) & (query_shard < shard_total)
    same_doc = key_doc[None, :] == query_doc[:, None]
    return same_doc & (key_pos[None, :] <= query_pos[:, None]) & inside


def attention_layer(doc_ids, shard_index, attn_queries, attn_keys, attn_values, attn_cot):
    query_loc, key_loc, value_loc, cot_loc = (
        lax.all_to_all(attn_queries, "chan", split_axis=1, concat_axis=0, tiled=True),
        lax.all_to_all(attn_keys, "chan", split_axis=1, concat_axis=0, tiled=True),
        lax.all_to_all(attn_values, "chan", split_axis=1, concat_axis=0, tiled=True),
        lax.all_to_all(attn_cot, "chan", split_axis=1, concat_axis=0, tiled=True),
    )
    row_count = query_loc.shape[0]
    head_count = query_loc.shape[1] // HEAD_DIM
    head_shape = (row_count, head_count, HEAD_DIM)
    query_heads = query_loc.reshape(head_shape)
    key_heads = key_loc.reshape(head_shape)
    value_heads = value_loc.reshape(head_shape)
    cot_heads = cot_loc.reshape(head_shape)
    shard_total = lax.axis_size("seq")
    score_scale = HEAD_DIM ** (-0.5)

    def score_block(key_block, pair_mask):
        raw_scores = (
            jnp.einsum("qhe,khe->hqk", query_heads, key_block, preferred_element_type=jnp.float32)
            * score_scale
        )
        return jnp.where(pair_mask[None], raw_scores, NEG)

    def mix_block(weight_block, value_block):
        return jnp.einsum(
            "hqk,khe->qhe", weight_block, value_block, preferred_element_type=jnp.float32
        )

    def weight_grads(value_block):
        return jnp.einsum(
            "qhe,khe->hqk", cot_heads, value_block, preferred_element_type=jnp.float32
        )

    def query_terms(dscore_block, key_block):
        return jnp.einsum(
            "hqk,khe->qhe", dscore_block, key_block, preferred_element_type=jnp.float32
        )

    held_keys = []
    held_values = []
    needs = []
    key_block, value_block = (key_heads, value_heads)
    scores = []
    for offset in range(SPAN_SH + 1):
        if offset > 0:
            key_block, value_block = shifted((key_block, value_block), "seq", 1)
        pair_mask = allowed_pairs(
            doc_ids, shard_index, shard_index - offset, row_count, shard_total
        )
        needed = jnp.any(pair_mask)
        held_keys.append(key_block)
        held_values.append(value_block)
        needs.append(needed)
        scores.append(guarded(score_block, (key_block, pair_mask)))
    row_peak = reduce(jnp.maximum, [jnp.max(block_scores, axis=2) for block_scores in scores])
    denominator = reduce(
        jnp.add,
        [jnp.sum(jnp.exp(block_scores - row_peak[..., None]), axis=2) for block_scores in scores],
    )
    weights = [
        (jnp.exp(block_scores - row_peak[..., None]) / denominator[..., None]).astype(jnp.bfloat16)
        for block_scores in scores
    ]
    attn_sum = reduce(
        jnp.add,
        [
            guarded(mix_block, (weights[offset], held_values[offset]))
            for offset in range(SPAN_SH + 1)
        ],
    )
    attn_out = attn_sum.astype(jnp.bfloat16).reshape(row_count, -1)
    dweights = [guarded(weight_grads, (held_values[offset],)) for offset in range(SPAN_SH + 1)]
    rowdot = reduce(
        jnp.add,
        [
            jnp.sum(weights[offset].astype(jnp.float32) * dweights[offset], axis=2)
            for offset in range(SPAN_SH + 1)
        ],
    )
    dscores = [
        (weights[offset].astype(jnp.float32) * (dweights[offset] - rowdot[..., None])).astype(
            jnp.bfloat16
        )
        for offset in range(SPAN_SH + 1)
    ]
    query_sum = reduce(
        jnp.add,
        [
            guarded(query_terms, (dscores[offset], held_keys[offset]))
            for offset in range(SPAN_SH + 1)
        ],
    )
    query_grad = (score_scale * query_sum).astype(jnp.bfloat16).reshape(row_count, -1)

    def key_terms(dscore_block, weight_block):
        key_part = score_scale * jnp.einsum(
            "hqk,qhe->khe", dscore_block, query_heads, preferred_element_type=jnp.float32
        )
        value_part = jnp.einsum(
            "hqk,qhe->khe", weight_block, cot_heads, preferred_element_type=jnp.float32
        )
        return (key_part, value_part)

    terms = [
        guarded(key_terms, (dscores[offset], weights[offset])) for offset in range(SPAN_SH + 1)
    ]
    grad_keys, grad_values = terms[SPAN_SH]
    for offset in range(SPAN_SH - 1, -1, -1):
        grad_keys, grad_values = shifted((grad_keys, grad_values), "seq", -1)
        grad_keys = grad_keys + terms[offset][0]
        grad_values = grad_values + terms[offset][1]
    key_grad = grad_keys.astype(jnp.bfloat16).reshape(row_count, -1)
    value_grad = grad_values.astype(jnp.bfloat16).reshape(row_count, -1)
    return (attn_out, query_grad, key_grad, value_grad)


def on_device(doc_ids, attn_queries, attn_keys, attn_values, attn_cot):
    shard_index = lax.axis_index("seq")
    attn_out, query_grad, key_grad, value_grad = attention_layer(
        doc_ids, shard_index, attn_queries, attn_keys, attn_values, attn_cot
    )
    return (attn_out, query_grad, key_grad, value_grad)


def solution(mesh):
    in_specs = (
        P(),
        P(("seq", "chan"), None),
        P(("seq", "chan"), None),
        P(("seq", "chan"), None),
        P(("seq", "chan"), None),
    )
    out_specs = (P("seq", "chan"), P("seq", "chan"), P("seq", "chan"), P("seq", "chan"))
    return jax.shard_map(
        on_device, mesh=mesh, in_specs=in_specs, out_specs=out_specs, check_vma=False
    )
```

profile of v0, /device:TPU:1, one launch (start us, length us, event | category | flops | bytes accessed | tf_op | source)
XLA Modules:
  0.0 355.0 jit_solution(18031108016275790375)
XLA Ops:
  0.6 2.4 copy.147
  3.0 5.9 %all-to-all-start.1 = ((bf16[64,4,2048]{2,0,1:T(8,128)(2,1)}), bf16[64,4,2048]{2,0,1:T(8,128)(2,1)S(1)}, u32[]{:S(2)}, u32[]{:S(2)}) async-start(bf16[64,4,2048]{2,0,1:T(8,128)(2,1)} %bitcast.120), calls=%async_computation.1 | async-start | bytes 2097152 | tf_op jit(solution)/shard_map/all_to_all | solution.py:39
  9.9 13.1 %all-to-all-done.1 = bf16[64,4,2048]{2,0,1:T(8,128)(2,1)S(1)} async-done(((bf16[64,4,2048]{2,0,1:T(8,128)(2,1)}), bf16[64,4,2048]{2,0,1:T(8,128)(2,1)S(1)}, u32[]{:S(2)}, u32[]{:S(2)}) %all-to-all-start.1) | async-done | bytes 1048608 | tf_op jit(solution)/shard_map/all_to_all | solution.py:39
  23.1 3.5 all-to-all-start.2
  27.6 12.2 %all-to-all-done.2 = bf16[64,4,2048]{2,0,1:T(8,128)(2,1)S(1)} async-done(((bf16[64,4,2048]{2,0,1:T(8,128)(2,1)}), bf16[64,4,2048]{2,0,1:T(8,128)(2,1)S(1)}, u32[]{:S(2)}, u32[]{:S(2)}) %all-to-all-start.2) | async-done | bytes 1048608 | tf_op jit(solution)/shard_map/all_to_all | solution.py:40
  40.8 3.5 all-to-all-start
  45.8 5.8 %collective-permute-start = (bf16[256,16,128]{2,0,1:T(8,128)(2,1)}, bf16[256,16,128]{2,0,1:T(8,128)(2,1)}, u32[]{:S(2)}, u32[]{:S(2)}) collective-permute-start(bf16[256,16,128]{2,0,1:T(8,128)(2,1)} %copy.71), channel_id=1, source_target_pairs={{0,4},{4,8},{8,12},{12,16},{16,20},{20,24},{24,28},{28,32},{32,36}... | collective-permute-start | bytes 3145736 | tf_op jit(solution)/shard_map/ppermute | solution.py:18
  55.3 2.3 copy.145
  57.6 4.5 %all-to-all-start.3 = ((bf16[64,4,2048]{2,0,1:T(8,128)(2,1)}), bf16[64,4,2048]{2,0,1:T(8,128)(2,1)S(1)}, u32[]{:S(2)}, u32[]{:S(2)}) async-start(bf16[64,4,2048]{2,0,1:T(8,128)(2,1)} %bitcast.118), calls=%async_computation.3 | async-start | bytes 2097152 | tf_op jit(solution)/shard_map/all_to_all | solution.py:41
  63.6 4.4 %collective-permute-start.1 = (bf16[256,16,128]{2,0,1:T(8,128)(2,1)}, bf16[256,16,128]{2,0,1:T(8,128)(2,1)}, u32[]{:S(2)}, u32[]{:S(2)}) collective-permute-start(bf16[256,16,128]{2,0,1:T(8,128)(2,1)} %collective-permute-done), channel_id=1, source_target_pairs={{0,4},{4,8},{8,12},{12,16},{16,20},{20,24},{24,28},{28,32},{32,36}... | collective-permute-start | bytes 3145736 | tf_op jit(solution)/shard_map/ppermute | solution.py:18
  71.5 4.0 %all-to-all-done.3 = bf16[64,4,2048]{2,0,1:T(8,128)(2,1)S(1)} async-done(((bf16[64,4,2048]{2,0,1:T(8,128)(2,1)}), bf16[64,4,2048]{2,0,1:T(8,128)(2,1)S(1)}, u32[]{:S(2)}, u32[]{:S(2)}) %all-to-all-start.3) | async-done | bytes 1048608 | tf_op jit(solution)/shard_map/all_to_all | solution.py:41
  78.3 5.7 %collective-permute-start.5 = (bf16[256,16,128]{0,2,1:T(8,128)(2,1)}, bf16[256,16,128]{0,2,1:T(8,128)(2,1)S(1)}, u32[]{:S(2)}, u32[]{:S(2)}) collective-permute-start(bf16[256,16,128]{0,2,1:T(8,128)(2,1)} %collective-permute-done.4), channel_id=1, source_target_pairs={{0,4},{4,8},{8,12},{12,16},{16,20},{20,24},{24,28},{28,32},{32,36}... | collective-permute-start | bytes 3145736 | tf_op jit(solution)/shard_map/ppermute | solution.py:18
  84.0 3.9 %fusion.27 = f32[16,256,256]{1,2,0:T(8,128)} fusion(bf16[256,16,128]{0,2,1:T(8,128)(2,1)S(1)} %copy.95, bf16[256,16,128]{0,2,1:T(8,128)(2,1)} %copy.53), kind=kOutput, calls=%fused_computation.81 | convolution fusion | flops 268435456 | bytes 6291456 | tf_op jit(solution)/shard_map/qhe,khe->hqk/dot_general | solution.py:66
  90.8 2.1 fusion.11
  92.9 4.4 %collective-permute-done.5 = bf16[256,16,128]{0,2,1:T(8,128)(2,1)S(1)} collective-permute-done((bf16[256,16,128]{0,2,1:T(8,128)(2,1)}, bf16[256,16,128]{0,2,1:T(8,128)(2,1)S(1)}, u32[]{:S(2)}, u32[]{:S(2)}) %collective-permute-start.5) | collective-permute-done | bytes 1048608 | tf_op jit(solution)/shard_map/ppermute | solution.py:18
  97.4 4.3 %collective-permute-start.6 = (bf16[256,16,128]{0,2,1:T(8,128)(2,1)S(1)}, bf16[256,16,128]{0,2,1:T(8,128)(2,1)S(1)}, u32[]{:S(2)}, u32[]{:S(2)}) collective-permute-start(bf16[256,16,128]{0,2,1:T(8,128)(2,1)S(1)} %collective-permute-done.5), channel_id=1, source_target_pairs={{0,4},{4,8},{8,12},{12,16},{16,20},{20,24},{24,28},{28,32},{32,36}... | collective-permute-start | bytes 3145736 | tf_op jit(solution)/shard_map/ppermute | solution.py:18
  101.6 4.0 %fusion.28 = f32[16,256,256]{1,2,0:T(8,128)} fusion(bf16[256,16,128]{0,2,1:T(8,128)(2,1)S(1)} %copy.95, bf16[256,16,128]{0,2,1:T(8,128)(2,1)} %collective-permute-done.4), kind=kOutput, calls=%fused_computation.82 | convolution fusion | flops 268435456 | bytes 6291456 | tf_op jit(solution)/shard_map/qhe,khe->hqk/dot_general | solution.py:66
  105.6 2.1 fusion.12
  108.6 4.3 %collective-permute-start.3 = (bf16[256,16,128]{2,0,1:T(8,128)(2,1)S(1)}, bf16[256,16,128]{2,0,1:T(8,128)(2,1)S(1)}, u32[]{:S(2)}, u32[]{:S(2)}) collective-permute-start(bf16[256,16,128]{2,0,1:T(8,128)(2,1)S(1)} %collective-permute-done.2), channel_id=1, source_target_pairs={{0,4},{4,8},{8,12},{12,16},{16,20},{20,24},{24,28},{28,32},{32,36}... | collective-permute-start | bytes 3145736 | tf_op jit(solution)/shard_map/ppermute | solution.py:18
  112.9 2.7 fusion.29
  115.6 4.1 %collective-permute-done.6 = bf16[256,16,128]{0,2,1:T(8,128)(2,1)S(1)} collective-permute-done((bf16[256,16,128]{0,2,1:T(8,128)(2,1)S(1)}, bf16[256,16,128]{0,2,1:T(8,128)(2,1)S(1)}, u32[]{:S(2)}, u32[]{:S(2)}) %collective-permute-start.6) | collective-permute-done | bytes 1048608 | tf_op jit(solution)/shard_map/ppermute | solution.py:18
  119.7 4.6 %collective-permute-start.7 = (bf16[256,16,128]{0,2,1:T(8,128)(2,1)S(1)}, bf16[256,16,128]{0,2,1:T(8,128)(2,1)}, u32[]{:S(2)}, u32[]{:S(2)}) collective-permute-start(bf16[256,16,128]{0,2,1:T(8,128)(2,1)S(1)} %collective-permute-done.6), channel_id=1, source_target_pairs={{0,4},{4,8},{8,12},{12,16},{16,20},{20,24},{24,28},{28,32},{32,36}... | collective-permute-start | bytes 3145736 | tf_op jit(solution)/shard_map/ppermute | solution.py:18
  124.3 2.7 fusion.30
  127.9 3.1 collective-permute-done.3
  132.0 5.0 %fusion.16 = (f32[16,256]{1,0:T(8,128)S(1)}, f32[16,256]{1,0:T(8,128)S(1)}, f32[16,256]{1,0:T(8,128)S(1)}, f32[16,256]{1,0:T(8,128)S(1)}, f32[16,256]{1,0:T(8,128)S(1)}) fusion(f32[16,256,256]{1,2,0:T(8,128)S(1)} %get-tuple-element.59, f32[16,256]{1,0:T(8,128)S(1)} %maximum_maximum_fusion, pred[256,256]{0,1:T(8,128)(4,1)S(1)} %get-tuple-element.45, ...), kind=kLoop, calls=%fused_computation.41 | loop fusion | flops 20951040 | bytes 21397504 | tf_op jit(solution)/shard_map/reduce_sum | solution.py:94
  137.0 5.2 %collective-permute-done.7 = bf16[256,16,128]{0,2,1:T(8,128)(2,1)} collective-permute-done((bf16[256,16,128]{0,2,1:T(8,128)(2,1)S(1)}, bf16[256,16,128]{0,2,1:T(8,128)(2,1)}, u32[]{:S(2)}, u32[]{:S(2)}) %collective-permute-start.7) | collective-permute-done | bytes 1048608 | tf_op jit(solution)/shard_map/ppermute | solution.py:18
  142.2 19.9 %fusion.8 = (f32[16,256]{1,0:T(8,128)S(1)}, bf16[16,256,256]{1,2,0:T(8,128)(2,1)}, f32[16,256]{1,0:T(8,128)S(1)}, bf16[16,256,256]{1,2,0:T(8,128)(2,1)}, f32[16,...) fusion(f32[16,256]{1,0:T(8,128)S(1)} %add_add_fusion.1, ...), kind=kOutput, calls=%fused_computation.18 | convolution fusion | flops 310358016 | bytes 54968320 | tf_op jit(solution)/shard_map/qhe,khe->hqk/dot_general | solution.py:66
  162.1 3.8 %convolution_bitcast_fusion = f32[256,16,128]{2,0,1:T(8,128)} fusion(bf16[16,256,256]{1,2,0:T(8,128)(2,1)} %get-tuple-element.26, bf16[256,16,128]{0,2,1:T(8,128)(2,1)S(1)} %copy.95), kind=kOutput, calls=%fused_computation.58 | convolution fusion | flops 268435456 | bytes 5242880 | tf_op jit(solution)/shard_map/hqk,qhe->khe/dot_general | solution.py:135
  167.9 13.2 %fusion.9 = (bf16[16,256,256]{1,2,0:T(8,128)(2,1)}, bf16[16,256,256]{1,2,0:T(8,128)(2,1)}, bf16[16,256,256]{1,2,0:T(8,128)(2,1)}, bf16[16,256,256]{1,2,0:T(8,128)(2,1)S(1)}, bf16[16,256,256]{1,2,0:T(8,128)(2,1)S(1)}) fusion(bf16[16,256,256]{1,2,0:T(8,128)(2,1)} %get-tuple-element.26, f32[16,256,256]{1,2,0:T(8,128)} %get-tuple-element.60, ...), kind=kLoop, calls=%fused_computation.19 | loop fusion | flops 20971520 | bytes 41959424 | tf_op jit(solution)/shard_map/convert_element_type | solution.py:117
  181.1 3.2 multiply_bitcast_fusion
  184.3 2.1 collective-permute-start.8
  187.2 7.2 %collective-permute-done.12 = f32[256,16,128]{2,0,1:T(8,128)} collective-permute-done((f32[256,16,128]{2,0,1:T(8,128)}, f32[256,16,128]{2,0,1:T(8,128)}, u32[]{:S(2)}, u32[]{:S(2)}) %collective-permute-start.12) | collective-permute-done | bytes 2097184 | tf_op jit(solution)/shard_map/ppermute | solution.py:18
  194.4 2.3 bitcast_add_fusion.3
  198.6 18.1 %collective-permute-done.8 = f32[256,16,128]{0,2,1:T(8,128)S(1)} collective-permute-done((f32[256,16,128]{0,2,1:T(8,128)S(1)}, f32[256,16,128]{0,2,1:T(8,128)S(1)}, u32[]{:S(2)}, u32[]{:S(2)}) %collective-permute-start.8) | collective-permute-done | bytes 2097184 | tf_op jit(solution)/shard_map/ppermute | solution.py:18
  220.3 3.1 fusion.40
  226.4 12.8 %collective-permute-done.13 = f32[256,16,128]{2,0,1:T(8,128)S(1)} collective-permute-done((f32[256,16,128]{2,0,1:T(8,128)S(1)}, f32[256,16,128]{2,0,1:T(8,128)S(1)}, u32[]{:S(2)}, u32[]{:S(2)}) %collective-permute-start.13) | collective-permute-done | bytes 2097184 | tf_op jit(solution)/shard_map/ppermute | solution.py:18
  241.5 20.2 %collective-permute-done.9 = f32[256,16,128]{0,2,1:T(8,128)S(1)} collective-permute-done((f32[256,16,128]{0,2,1:T(8,128)S(1)}, f32[256,16,128]{0,2,1:T(8,128)S(1)}, u32[]{:S(2)}, u32[]{:S(2)}) %collective-permute-start.9) | collective-permute-done | bytes 2097184 | tf_op jit(solution)/shard_map/ppermute | solution.py:18
  268.1 3.2 fusion.41
  272.3 11.9 %collective-permute-done.14 = f32[256,16,128]{2,0,1:T(8,128)S(1)} collective-permute-done((f32[256,16,128]{2,0,1:T(8,128)S(1)}, f32[256,16,128]{2,0,1:T(8,128)S(1)}, u32[]{:S(2)}, u32[]{:S(2)}) %collective-permute-start.14) | collective-permute-done | bytes 2097184 | tf_op jit(solution)/shard_map/ppermute | solution.py:18
  285.8 2.0 collective-permute-start.15
  287.8 18.8 %collective-permute-done.10 = f32[256,16,128]{0,2,1:T(8,128)S(1)} collective-permute-done((f32[256,16,128]{0,2,1:T(8,128)S(1)}, f32[256,16,128]{0,2,1:T(8,128)S(1)}, u32[]{:S(2)}, u32[]{:S(2)}) %collective-permute-start.10) | collective-permute-done | bytes 2097184 | tf_op jit(solution)/shard_map/ppermute | solution.py:18
  308.3 2.2 collective-permute-start.11
  313.7 2.5 fusion.43
  316.9 3.3 add_convert_fusion
  321.6 3.9 %fusion.36 = f32[16,256,128]{1,2,0:T(8,128)} fusion(bf16[16,256,256]{1,2,0:T(8,128)(2,1)} %copy-done.4, bf16[256,16,128]{0,2,1:T(8,128)(2,1)S(1)} %copy.89), kind=kOutput, calls=%fused_computation.90 | convolution fusion | flops 268435456 | bytes 5242880 | tf_op jit(solution)/shard_map/hqk,qhe->khe/dot_general | solution.py:132
  326.2 3.1 collective-permute-done.15
  332.4 2.3 copy.101
  334.7 17.0 %collective-permute-done.11 = f32[256,16,128]{0,2,1:T(8,128)} collective-permute-done((f32[256,16,128]{0,2,1:T(8,128)}, f32[256,16,128]{0,2,1:T(8,128)}, u32[]{:S(2)}, u32[]{:S(2)}) %collective-permute-start.11) | collective-permute-done | bytes 2097184 | tf_op jit(solution)/shard_map/ppermute | solution.py:18
  (114 shorter events, 58.0 us)
Async XLA Ops:
  0.6 8.3 %copy-start.26 = (bf16[64,8192]{1,0:T(8,128)(2,1)S(1)}, bf16[64,8192]{1,0:T(8,128)(2,1)}, u32[]{:S(2)}) copy-start(bf16[64,8192]{1,0:T(8,128)(2,1)} %param.8) | copy-start | bytes 3145732
  3.0 20.0 %all-to-all-start.1 = ((bf16[64,4,2048]{2,0,1:T(8,128)(2,1)}), bf16[64,4,2048]{2,0,1:T(8,128)(2,1)S(1)}, u32[]{:S(2)}, u32[]{:S(2)}) async-start(bf16[64,4,2048]{2,0,1:T(8,128)(2,1)} %bitcast.120), calls=%async_computation.1 | async-start | bytes 2097152 | tf_op jit(solution)/shard_map/all_to_all | solution.py:39
  8.9 17.7 %copy-start.27 = (bf16[64,8192]{1,0:T(8,128)(2,1)S(1)}, bf16[64,8192]{1,0:T(8,128)(2,1)}, u32[]{:S(2)}) copy-start(bf16[64,8192]{1,0:T(8,128)(2,1)} %param.6) | copy-start | bytes 3145732
  23.1 16.8 %all-to-all-start.2 = ((bf16[64,4,2048]{2,0,1:T(8,128)(2,1)}), bf16[64,4,2048]{2,0,1:T(8,128)(2,1)S(1)}, u32[]{:S(2)}, u32[]{:S(2)}) async-start(bf16[64,4,2048]{2,0,1:T(8,128)(2,1)} %bitcast.121), calls=%async_computation.2 | async-start | bytes 2097152 | tf_op jit(solution)/shard_map/all_to_all | solution.py:40
  40.8 16.9 %all-to-all-start = ((bf16[64,4,2048]{2,0,1:T(8,128)(2,1)}), bf16[64,4,2048]{2,0,1:T(8,128)(2,1)S(1)}, u32[]{:S(2)}, u32[]{:S(2)}) async-start(bf16[64,4,2048]{2,0,1:T(8,128)(2,1)} %bitcast.119), calls=%async_computation | async-start | bytes 2097152 | tf_op jit(solution)/shard_map/all_to_all | solution.py:38
  44.3 7.3 %copy-start.25 = (bf16[64,4,2048]{2,0,1:T(8,128)(2,1)S(1)}, bf16[64,4,2048]{2,0,1:T(8,128)(2,1)}, u32[]{:S(2)}) copy-start(bf16[64,4,2048]{2,0,1:T(8,128)(2,1)} %copy-done.24) | copy-start | bytes 3145732
  45.8 17.8 %collective-permute-start = (bf16[256,16,128]{2,0,1:T(8,128)(2,1)}, bf16[256,16,128]{2,0,1:T(8,128)(2,1)}, u32[]{:S(2)}, u32[]{:S(2)}) collective-permute-start(bf16[256,16,128]{2,0,1:T(8,128)(2,1)} %copy.71), channel_id=1, source_target_pairs={{0,4},{4,8},{8,12},{12,16},{16,20},{20,24},{24,28},{28,32},{32,36}... | collective-permute-start | bytes 3145736 | tf_op jit(solution)/shard_map/ppermute | solution.py:18
  53.4 24.9 %collective-permute-start.4 = (bf16[256,16,128]{0,2,1:T(8,128)(2,1)}, bf16[256,16,128]{0,2,1:T(8,128)(2,1)}, u32[]{:S(2)}, u32[]{:S(2)}) collective-permute-start(bf16[256,16,128]{0,2,1:T(8,128)(2,1)} %copy.53), channel_id=1, source_target_pairs={{0,4},{4,8},{8,12},{12,16},{16,20},{20,24},{24,28},{28,32},{32,36}... | collective-permute-start | bytes 3145736 | tf_op jit(solution)/shard_map/ppermute | solution.py:18
  57.6 17.8 %all-to-all-start.3 = ((bf16[64,4,2048]{2,0,1:T(8,128)(2,1)}), bf16[64,4,2048]{2,0,1:T(8,128)(2,1)S(1)}, u32[]{:S(2)}, u32[]{:S(2)}) async-start(bf16[64,4,2048]{2,0,1:T(8,128)(2,1)} %bitcast.118), calls=%async_computation.3 | async-start | bytes 2097152 | tf_op jit(solution)/shard_map/all_to_all | solution.py:41
  63.6 25.2 %collective-permute-start.1 = (bf16[256,16,128]{2,0,1:T(8,128)(2,1)}, bf16[256,16,128]{2,0,1:T(8,128)(2,1)}, u32[]{:S(2)}, u32[]{:S(2)}) collective-permute-start(bf16[256,16,128]{2,0,1:T(8,128)(2,1)} %collective-permute-done), channel_id=1, source_target_pairs={{0,4},{4,8},{8,12},{12,16},{16,20},{20,24},{24,28},{28,32},{32,36}... | collective-permute-start | bytes 3145736 | tf_op jit(solution)/shard_map/ppermute | solution.py:18
  78.3 19.0 %collective-permute-start.5 = (bf16[256,16,128]{0,2,1:T(8,128)(2,1)}, bf16[256,16,128]{0,2,1:T(8,128)(2,1)S(1)}, u32[]{:S(2)}, u32[]{:S(2)}) collective-permute-start(bf16[256,16,128]{0,2,1:T(8,128)(2,1)} %collective-permute-done.4), channel_id=1, source_target_pairs={{0,4},{4,8},{8,12},{12,16},{16,20},{20,24},{24,28},{28,32},{32,36}... | collective-permute-start | bytes 3145736 | tf_op jit(solution)/shard_map/ppermute | solution.py:18
  88.9 43.1 %copy-start.10 = (f32[16,256,256]{1,2,0:T(8,128)}, f32[16,256,256]{1,2,0:T(8,128)S(1)}, u32[]{:S(2)}) copy-start(f32[16,256,256]{1,2,0:T(8,128)S(1)} %get-tuple-element.57) | copy-start | bytes 12582916
  88.9 19.7 %collective-permute-start.2 = (bf16[256,16,128]{2,0,1:T(8,128)(2,1)}, bf16[256,16,128]{2,0,1:T(8,128)(2,1)S(1)}, u32[]{:S(2)}, u32[]{:S(2)}) collective-permute-start(bf16[256,16,128]{2,0,1:T(8,128)(2,1)} %collective-permute-done.1), channel_id=1, source_target_pairs={{0,4},{4,8},{8,12},{12,16},{16,20},{20,24},{24,28},{28,32},{32,36}... | collective-permute-start | bytes 3145736 | tf_op jit(solution)/shard_map/ppermute | solution.py:18
  92.9 39.1 %copy-start.11 = (f32[16,256,256]{1,2,0:T(8,128)}, f32[16,256,256]{1,2,0:T(8,128)S(1)}, u32[]{:S(2)}) copy-start(f32[16,256,256]{1,2,0:T(8,128)S(1)} %get-tuple-element.59) | copy-start | bytes 12582916
  97.4 15.5 %copy-start.21 = (bf16[256,16,128]{0,2,1:T(8,128)(2,1)}, bf16[256,16,128]{0,2,1:T(8,128)(2,1)S(1)}, u32[]{:S(2)}) copy-start(bf16[256,16,128]{0,2,1:T(8,128)(2,1)S(1)} %collective-permute-done.5) | copy-start | bytes 3145732
  97.4 22.4 %collective-permute-start.6 = (bf16[256,16,128]{0,2,1:T(8,128)(2,1)S(1)}, bf16[256,16,128]{0,2,1:T(8,128)(2,1)S(1)}, u32[]{:S(2)}, u32[]{:S(2)}) collective-permute-start(bf16[256,16,128]{0,2,1:T(8,128)(2,1)S(1)} %collective-permute-done.5), channel_id=1, source_target_pairs={{0,4},{4,8},{8,12},{12,16},{16,20},{20,24},{24,28},{28,32},{32,36}... | collective-permute-start | bytes 3145736 | tf_op jit(solution)/shard_map/ppermute | solution.py:18
  107.7 24.3 %copy-start.12 = (f32[16,256,256]{1,2,0:T(8,128)}, f32[16,256,256]{1,2,0:T(8,128)S(1)}, u32[]{:S(2)}) copy-start(f32[16,256,256]{1,2,0:T(8,128)S(1)} %get-tuple-element.55) | copy-start | bytes 12582916
  108.6 18.4 %copy-start.17 = (bf16[256,16,128]{2,0,1:T(8,128)(2,1)}, bf16[256,16,128]{2,0,1:T(8,128)(2,1)S(1)}, u32[]{:S(2)}) copy-start(bf16[256,16,128]{2,0,1:T(8,128)(2,1)S(1)} %collective-permute-done.2) | copy-start | bytes 3145732
  108.6 22.4 %collective-permute-start.3 = (bf16[256,16,128]{2,0,1:T(8,128)(2,1)S(1)}, bf16[256,16,128]{2,0,1:T(8,128)(2,1)S(1)}, u32[]{:S(2)}, u32[]{:S(2)}) collective-permute-start(bf16[256,16,128]{2,0,1:T(8,128)(2,1)S(1)} %collective-permute-done.2), channel_id=1, source_target_pairs={{0,4},{4,8},{8,12},{12,16},{16,20},{20,24},{24,28},{28,32},{32,36}... | collective-permute-start | bytes 3145736 | tf_op jit(solution)/shard_map/ppermute | solution.py:18
  119.7 7.3 %copy-start.23 = (bf16[256,16,128]{0,2,1:T(8,128)(2,1)}, bf16[256,16,128]{0,2,1:T(8,128)(2,1)S(1)}, u32[]{:S(2)}) copy-start(bf16[256,16,128]{0,2,1:T(8,128)(2,1)S(1)} %collective-permute-done.6) | copy-start | bytes 3145732
  119.7 22.5 %collective-permute-start.7 = (bf16[256,16,128]{0,2,1:T(8,128)(2,1)S(1)}, bf16[256,16,128]{0,2,1:T(8,128)(2,1)}, u32[]{:S(2)}, u32[]{:S(2)}) collective-permute-start(bf16[256,16,128]{0,2,1:T(8,128)(2,1)S(1)} %collective-permute-done.6), channel_id=1, source_target_pairs={{0,4},{4,8},{8,12},{12,16},{16,20},{20,24},{24,28},{28,32},{32,36}... | collective-permute-start | bytes 3145736 | tf_op jit(solution)/shard_map/ppermute | solution.py:18
  127.9 4.1 %copy-start.13 = (f32[16,256,256]{1,2,0:T(8,128)}, f32[16,256,256]{1,2,0:T(8,128)S(1)}, u32[]{:S(2)}) copy-start(f32[16,256,256]{1,2,0:T(8,128)S(1)} %get-tuple-element.53) | copy-start | bytes 12582916
  131.9 5.0 %copy-start.14 = (f32[16,256,256]{1,2,0:T(8,128)}, f32[16,256,256]{1,2,0:T(8,128)S(1)}, u32[]{:S(2)}) copy-start(f32[16,256,256]{1,2,0:T(8,128)S(1)} %get-tuple-element.51) | copy-start | bytes 12582916
  162.1 5.7 %copy-start.28 = (f32[16,256]{1,0:T(8,128)S(1)}, f32[16,256]{1,0:T(8,128)}, u32[]{:S(2)}) copy-start(f32[16,256]{1,0:T(8,128)} %get-tuple-element.31) | copy-start | bytes 49156
  162.1 5.7 %copy-start.29 = (f32[16,256]{1,0:T(8,128)S(1)}, f32[16,256]{1,0:T(8,128)}, u32[]{:S(2)}) copy-start(f32[16,256]{1,0:T(8,128)} %get-tuple-element.33) | copy-start | bytes 49156
  162.1 5.7 %copy-start = (bf16[16,256,256]{1,2,0:T(8,128)(2,1)S(1)}, bf16[16,256,256]{1,2,0:T(8,128)(2,1)}, u32[]{:S(2)}) copy-start(bf16[16,256,256]{1,2,0:T(8,128)(2,1)} %get-tuple-element.32) | copy-start | bytes 6291460
  162.1 5.7 %copy-start.1 = (bf16[16,256,256]{1,2,0:T(8,128)(2,1)S(1)}, bf16[16,256,256]{1,2,0:T(8,128)(2,1)}, u32[]{:S(2)}) copy-start(bf16[16,256,256]{1,2,0:T(8,128)(2,1)} %get-tuple-element.34) | copy-start | bytes 6291460
  165.9 28.5 %collective-permute-start.12 = (f32[256,16,128]{2,0,1:T(8,128)}, f32[256,16,128]{2,0,1:T(8,128)}, u32[]{:S(2)}, u32[]{:S(2)}) collective-permute-start(f32[256,16,128]{2,0,1:T(8,128)} %convolution_bitcast_fusion), channel_id=1, source_target_pairs={{4,0},{8,4},{12,8},{16,12},{20,16},{24,20},{28,24},{32,28},{36,32}... | collective-permute-start | bytes 6291464 | tf_op jit(solution)/shard_map/ppermute | solution.py:18
  181.1 44.8 %copy-start.4 = (bf16[16,256,256]{1,2,0:T(8,128)(2,1)}, bf16[16,256,256]{1,2,0:T(8,128)(2,1)S(1)}, u32[]{:S(2)}) copy-start(bf16[16,256,256]{1,2,0:T(8,128)(2,1)S(1)} %get-tuple-element.44) | copy-start | bytes 6291460
  181.1 5.4 %copy-start.5 = (bf16[16,256,256]{1,2,0:T(8,128)(2,1)S(1)}, bf16[16,256,256]{1,2,0:T(8,128)(2,1)}, u32[]{:S(2)}) copy-start(bf16[16,256,256]{1,2,0:T(8,128)(2,1)} %get-tuple-element.28) | copy-start | bytes 6291460
  184.3 32.5 %collective-permute-start.8 = (f32[256,16,128]{0,2,1:T(8,128)S(1)}, f32[256,16,128]{0,2,1:T(8,128)S(1)}, u32[]{:S(2)}, u32[]{:S(2)}) collective-permute-start(f32[256,16,128]{0,2,1:T(8,128)S(1)} %multiply_bitcast_fusion), channel_id=1, source_target_pairs={{4,0},{8,4},{12,8},{16,12},{20,16},{24,20},{28,24},{32,28},{36,32}... | collective-permute-start | bytes 6291464 | tf_op jit(solution)/shard_map/ppermute | solution.py:18
  196.7 42.5 %collective-permute-start.13 = (f32[256,16,128]{2,0,1:T(8,128)S(1)}, f32[256,16,128]{2,0,1:T(8,128)S(1)}, u32[]{:S(2)}, u32[]{:S(2)}) collective-permute-start(f32[256,16,128]{2,0,1:T(8,128)S(1)} %bitcast_add_fusion.3), channel_id=1, source_target_pairs={{4,0},{8,4},{12,8},{16,12},{20,16},{24,20},{28,24},{32,28},{36,32}... | collective-permute-start | bytes 6291464 | tf_op jit(solution)/shard_map/ppermute | solution.py:18
  216.8 2.8 copy-start.3
  217.6 44.1 %collective-permute-start.9 = (f32[256,16,128]{0,2,1:T(8,128)S(1)}, f32[256,16,128]{0,2,1:T(8,128)S(1)}, u32[]{:S(2)}, u32[]{:S(2)}) collective-permute-start(f32[256,16,128]{0,2,1:T(8,128)S(1)} %bitcast_add_fusion.7), channel_id=1, source_target_pairs={{4,0},{8,4},{12,8},{16,12},{20,16},{24,20},{28,24},{32,28},{36,32}... | collective-permute-start | bytes 6291464 | tf_op jit(solution)/shard_map/ppermute | solution.py:18
  220.3 3.1 copy-start.7
  223.4 1.6 copy-start.6
  239.6 44.6 %collective-permute-start.14 = (f32[256,16,128]{2,0,1:T(8,128)S(1)}, f32[256,16,128]{2,0,1:T(8,128)S(1)}, u32[]{:S(2)}, u32[]{:S(2)}) collective-permute-start(f32[256,16,128]{2,0,1:T(8,128)S(1)} %bitcast_add_fusion.2), channel_id=1, source_target_pairs={{4,0},{8,4},{12,8},{16,12},{20,16},{24,20},{28,24},{32,28},{36,32}... | collective-permute-start | bytes 6291464 | tf_op jit(solution)/shard_map/ppermute | solution.py:18
  262.0 44.6 %collective-permute-start.10 = (f32[256,16,128]{0,2,1:T(8,128)S(1)}, f32[256,16,128]{0,2,1:T(8,128)S(1)}, u32[]{:S(2)}, u32[]{:S(2)}) collective-permute-start(f32[256,16,128]{0,2,1:T(8,128)S(1)} %bitcast_add_fusion.6), channel_id=1, source_target_pairs={{4,0},{8,4},{12,8},{16,12},{20,16},{24,20},{28,24},{32,28},{36,32}... | collective-permute-start | bytes 6291464 | tf_op jit(solution)/shard_map/ppermute | solution.py:18
  265.7 1.8 copy-start.18
  268.1 3.2 copy-start.9
  268.1 3.2 copy-start.20
  285.8 24.7 %copy-start.22 = (bf16[256,16,128]{0,2,1:T(8,128)(2,1)S(1)}, bf16[256,16,128]{0,2,1:T(8,128)(2,1)}, u32[]{:S(2)}) copy-start(bf16[256,16,128]{0,2,1:T(8,128)(2,1)} %copy-done.21) | copy-start | bytes 3145732
  285.8 43.4 %collective-permute-start.15 = (f32[256,16,128]{2,0,1:T(8,128)}, f32[256,16,128]{2,0,1:T(8,128)}, u32[]{:S(2)}, u32[]{:S(2)}) collective-permute-start(f32[256,16,128]{2,0,1:T(8,128)} %bitcast_add_fusion.1), channel_id=1, source_target_pairs={{4,0},{8,4},{12,8},{16,12},{20,16},{24,20},{28,24},{32,28},{36,32}... | collective-permute-start | bytes 6291464 | tf_op jit(solution)/shard_map/ppermute | solution.py:18
  308.3 43.4 %collective-permute-start.11 = (f32[256,16,128]{0,2,1:T(8,128)}, f32[256,16,128]{0,2,1:T(8,128)}, u32[]{:S(2)}, u32[]{:S(2)}) collective-permute-start(f32[256,16,128]{0,2,1:T(8,128)} %bitcast_add_fusion.5), channel_id=1, source_target_pairs={{4,0},{8,4},{12,8},{16,12},{20,16},{24,20},{28,24},{32,28},{36,32}... | collective-permute-start | bytes 6291464 | tf_op jit(solution)/shard_map/ppermute | solution.py:18
  313.7 2.5 copy-start.8
  313.7 3.2 copy-start.16
  321.6 3.9 %copy-start.2 = (bf16[16,256,256]{1,2,0:T(8,128)(2,1)S(1)}, bf16[16,256,256]{1,2,0:T(8,128)(2,1)}, u32[]{:S(2)}) copy-start(bf16[16,256,256]{1,2,0:T(8,128)(2,1)} %get-tuple-element.34) | copy-start | bytes 6291460
  331.1 20.6 %copy-start.15 = (f32[16,256,128]{1,2,0:T(8,128)S(1)}, f32[16,256,128]{1,2,0:T(8,128)}, u32[]{:S(2)}) copy-start(f32[16,256,128]{1,2,0:T(8,128)} %fusion.36) | copy-start | bytes 6291460
  (2 other events, 2.0 us)
where the time goes:
time: 358 us; the launch traced here: 355 us
  waiting for transfers between devices  157 us (44%)
  matrix products  77.3 us (22%)
  starting transfers between devices  66.1 us (18%)
  other arithmetic  27.3 us (8%)
  local copies, waits for them, and re-layouts  26.2 us (7%)
    ppermute x16, waiting for transfers between devices, shifted(): return lax.ppermute(value, axis, pairs)  128 us
    ppermute x16, starting transfers between devices, shifted(): return lax.ppermute(value, axis, pairs)  48.8 us
    dot_general x5, matrix products, weight_grads(): jnp.einsum('qhe,khe->hqk', cot_heads, value_block, preferred_element_type...  33.2 us
    dot_general x5, matrix products, mix_block(): jnp.einsum('hqk,khe->qhe', weight_block, value_block, preferred_element_t...  13.8 us
    convert_element_type x1, other arithmetic, attention_layer(): (weights[offset].astype(jnp.float32) * (dweights[offset] - rowdot[..., No...  13.2 us
    all_to_all x1, waiting for transfers between devices, attention_layer(): lax.all_to_all(attn_keys, 'chan', split_axis=1, concat_axis=0, tiled=True)  13.1 us
    all_to_all x1, waiting for transfers between devices, attention_layer(): lax.all_to_all(attn_values, 'chan', split_axis=1, concat_axis=0, tiled=True)  12.2 us
    unnamed x68, local copies, waits for them, and re-layouts  12 us
  transfers between devices with their start and end apart: 20, of which 17 were waited for; matrix products, arithmetic and copies ran while one was open for 28% of the time, Pallas kernels for 0%

commit v1 on v0

v1 whole, which is shorter than its diff:
```python
import functools

import jax
import jax.numpy as jnp
from jax import lax
from jax.experimental import pallas as pl
from jax.experimental.pallas import tpu as pltpu
from jax.sharding import PartitionSpec as P

MESH = pl.DeviceIdType.MESH
HEAD = 128
ROW = 8
CHAN = 4
TOK = 256
PIECE = 64
SPAN = ROW * TOK
HALO = 1024
KEYS = SPAN + HALO
PAIR = 2 * HEAD
LOG2E = 1.4426950408889634
NEG = -1e30
F32 = jnp.float32
BF16 = jnp.bfloat16
DOCS = 16


def place():
    shard = lax.axis_index("seq")
    plane = lax.axis_index("chan")
    spot = lax.rem(shard, ROW)
    return shard - spot, spot, plane


def wait_bytes(ref, sem):
    pltpu.make_async_copy(ref, ref, sem).wait()


def gather_kernel(rows_total, q, k, v, g, kv, qg, send_sem, recv_sem, up_send, up_recv):
    base, spot, plane = place()
    half = spot // 4
    above = (lax.rem(base + ROW, rows_total) + spot, plane)
    below = (lax.rem(base + rows_total - ROW, rows_total) + spot, plane)
    bar = pltpu.get_barrier_semaphore()
    for i in range(ROW):
        for j in range(CHAN):
            if i or j:
                peer = (base + lax.rem(spot + i, ROW), lax.rem(plane + j, CHAN))
                pl.semaphore_signal(bar, inc=1, device_id=peer, device_id_type=MESH)
    pl.semaphore_signal(bar, inc=1, device_id=above, device_id_type=MESH)
    pl.semaphore_signal(bar, inc=1, device_id=below, device_id_type=MESH)
    pl.semaphore_wait(bar, ROW * CHAN + 1)

    start = spot * TOK + plane * PIECE

    def columns(i, j):
        pair = lax.rem(plane + j, CHAN) * ROW + lax.rem(spot + i, ROW)
        return pl.ds(pl.multiple_of(pair * PAIR, PAIR), PAIR)

    def send(src, dst, t):
        pltpu.make_async_copy(src.at[:, columns(0, 0)], dst, recv_sem.at[t, half]).start()
        for i in range(ROW):
            for j in range(CHAN):
                if i or j:
                    pltpu.make_async_remote_copy(
                        src_ref=src.at[:, columns(i, j)],
                        dst_ref=dst,
                        send_sem=send_sem.at[t],
                        recv_sem=recv_sem.at[t, half],
                        device_id=(base + lax.rem(spot + i, ROW), lax.rem(plane + j, CHAN)),
                        device_id_type=MESH,
                    ).start()

    def rows(offset):
        return pl.ds(pl.multiple_of(offset + start, PIECE), PIECE)

    def raise_half(t):
        wait_bytes(kv.at[t, pl.ds(2 * HALO, HALO), :], recv_sem.at[t, 1])
        up = pltpu.make_async_remote_copy(
            src_ref=kv.at[t, pl.ds(2 * HALO, HALO), :],
            dst_ref=kv.at[t, pl.ds(0, HALO), :],
            send_sem=up_send.at[t],
            recv_sem=up_recv.at[t],
            device_id=above,
            device_id_type=MESH,
        )
        up.start()
        return up

    send(k, kv.at[0, rows(HALO), :], 0)
    send(v, kv.at[1, rows(HALO), :], 1)
    up_keys = raise_half(0)
    send(q, qg.at[0, rows(0), :], 2)
    up_values = raise_half(1)
    send(g, qg.at[1, rows(0), :], 3)
    for t in range(2):
        wait_bytes(kv.at[t, pl.ds(HALO, HALO), :], recv_sem.at[t, 0])
        wait_bytes(qg.at[t, pl.ds(0, HALO), :], recv_sem.at[2 + t, 0])
        wait_bytes(qg.at[t, pl.ds(HALO, HALO), :], recv_sem.at[2 + t, 1])
    for t in range(4):
        wait_bytes(qg.at[0, pl.ds(0, (ROW * CHAN - 1) * PIECE), :], send_sem.at[t])
    up_keys.wait()
    up_values.wait()


def gather_inputs(rows_total, q, k, v, g):
    any_space = pl.BlockSpec(memory_space=pl.ANY)
    return pl.pallas_call(
        functools.partial(gather_kernel, rows_total),
        out_shape=(
            jax.ShapeDtypeStruct((2, KEYS, PAIR), BF16),
            jax.ShapeDtypeStruct((2, SPAN, PAIR), BF16),
        ),
        in_specs=[any_space] * 4,
        out_specs=(any_space, any_space),
        scratch_shapes=[
            pltpu.SemaphoreType.DMA((4,)),
            pltpu.SemaphoreType.DMA((4, 2)),
            pltpu.SemaphoreType.DMA((2,)),
            pltpu.SemaphoreType.DMA((2,)),
        ],
        compiler_params=pltpu.CompilerParams(collective_id=0, has_side_effects=True),
        name="gather_inputs",
    )(q, k, v, g)


def dot(a, b, ca, cb):
    return lax.dot_general(a, b, (((ca,), (cb,)), ((), ())), preferred_element_type=F32)


def attention_kernel(docs_s, docs, kv, qg, og, dkv, scores, weights, keys_t, values_t, dk_acc, dv_acc, limits):
    base = lax.axis_index("seq") // ROW * SPAN
    scale = HEAD ** -0.5
    log_scale = scale * LOG2E

    all_docs = docs[...]
    first_line = base // HEAD
    own = docs[pl.ds(pl.multiple_of(first_line, 16), SPAN // HEAD), :]
    starts = jnp.zeros_like(own)
    for d in range(1, DOCS):
        below = jnp.where(all_docs < d, 1.0, 0.0)
        count = jnp.sum(jnp.sum(below, axis=0, keepdims=True), axis=1, keepdims=True)
        starts = jnp.where(own == d, jnp.broadcast_to(count.astype(jnp.int32), own.shape), starts)
    limits[...] = starts - (base - HALO)

    for b in range(KEYS // TOK):
        span = pl.ds(b * TOK, TOK)
        keys_t[:, span] = kv[0, span, :].T
        values_t[:, span] = kv[1, span, :].T
    dk_acc[...] = jnp.zeros_like(dk_acc)
    dv_acc[...] = jnp.zeros_like(dv_acc)

    heads = [pl.ds(h * HEAD, HEAD) for h in range(2)]
    key_iota = lax.broadcasted_iota(jnp.int32, (TOK, TOK), 0)
    diagonal = key_iota <= lax.broadcasted_iota(jnp.int32, (TOK, TOK), 1)

    def one_block(b, carry):
        first = base + b * TOK
        doc = docs_s[first]
        reach = jnp.int32(0)
        for o in range(1, 5):
            spot = first - 1 - (o - 1) * TOK
            hit = (spot >= 0) & (docs_s[jnp.maximum(spot, 0)] == doc)
            reach = reach + hit.astype(jnp.int32)
        rows = pl.ds(pl.multiple_of(b * TOK, TOK), TOK)
        low = jnp.concatenate([limits[pl.ds(2 * b, 1), :], limits[pl.ds(2 * b + 1, 1), :]], axis=1)
        queries = [qg[0, rows, heads[h]] for h in range(2)]
        cots = [qg[1, rows, heads[h]] for h in range(2)]

        def key_rows(o):
            return pl.ds(pl.multiple_of((b + 4 - o) * TOK, TOK), TOK)

        def masked(o, h):
            raw = dot(kv[0, key_rows(o), heads[h]], queries[h], 1, 1)
            return jnp.where(key_iota + (b + 4 - o) * TOK >= low, raw, NEG)

        peaks = []
        for h in range(2):
            part = jnp.where(diagonal, masked(0, h), NEG)
            scores[h, 0] = part
            peaks.append(jnp.max(part, axis=0, keepdims=True))

        def sweep_scores(o, peaks):
            out = []
            for h in range(2):
                part = masked(o, h)
                scores[h, o] = part
                out.append(jnp.maximum(peaks[h], jnp.max(part, axis=0, keepdims=True)))
            return tuple(out)

        peaks = lax.fori_loop(1, reach + 1, sweep_scores, tuple(peaks))
        shifts = [peak * log_scale for peak in peaks]

        def sweep_weights(o, state):
            out = []
            for h in range(2):
                total, mixed = state[h]
                expo = jnp.exp2(scores[h, o] * log_scale - shifts[h])
                small = expo.astype(BF16)
                weights[h, o] = small
                total = total + jnp.sum(expo, axis=0, keepdims=True)
                mixed = mixed + dot(values_t[heads[h], key_rows(o)], small, 1, 0)
                out.append((total, mixed))
            return tuple(out)

        zero = (jnp.zeros((1, TOK), F32), jnp.zeros((HEAD, TOK), F32))
        state = lax.fori_loop(0, reach + 1, sweep_weights, (zero, zero))
        tails = []
        for h in range(2):
            total, mixed = state[h]
            inverse = 1.0 / total
            mixed = mixed * inverse
            og[0, rows, heads[h]] = mixed.T.astype(BF16)
            cot_t = (cots[h].astype(F32).T * inverse).astype(BF16)
            rowdot = jnp.sum(cot_t.astype(F32) * mixed, axis=0, keepdims=True)
            tails.append((cot_t, cot_t.T, rowdot))

        def sweep_grads(o, grads):
            out = []
            keys = key_rows(o)
            for h in range(2):
                cot_t, cot, rowdot = tails[h]
                weight = weights[h, o]
                dweight = dot(kv[1, keys, heads[h]], cot_t, 1, 0)
                dscore = (weight.astype(F32) * (dweight - rowdot)).astype(BF16)
                dv_acc[keys, heads[h]] += dot(weight, cot, 1, 0)
                dk_acc[keys, heads[h]] += dot(dscore, queries[h], 1, 0)
                out.append(grads[h] + dot(keys_t[heads[h], keys], dscore, 1, 0))
            return tuple(out)

        blank = jnp.zeros((HEAD, TOK), F32)
        grads = lax.fori_loop(0, reach + 1, sweep_grads, (blank, blank))
        for h in range(2):
            og[1, rows, heads[h]] = (grads[h] * scale).T.astype(BF16)
        return carry

    lax.fori_loop(0, ROW, one_block, 0)
    for b in range(KEYS // TOK):
        span = pl.ds(b * TOK, TOK)
        dkv[0, span, :] = (dk_acc[span, :] * scale).astype(BF16)
        dkv[1, span, :] = dv_acc[span, :].astype(BF16)


def attention(docs, kv, qg):
    vmem = pl.BlockSpec(memory_space=pltpu.VMEM)
    return pl.pallas_call(
        attention_kernel,
        out_shape=(
            jax.ShapeDtypeStruct((2, SPAN, PAIR), BF16),
            jax.ShapeDtypeStruct((2, KEYS, PAIR), BF16),
        ),
        in_specs=[pl.BlockSpec(memory_space=pltpu.SMEM), vmem, vmem, vmem],
        out_specs=(vmem, vmem),
        scratch_shapes=[
            pltpu.VMEM((2, 5, TOK, TOK), F32),
            pltpu.VMEM((2, 5, TOK, TOK), BF16),
            pltpu.VMEM((PAIR, KEYS), BF16),
            pltpu.VMEM((PAIR, KEYS), BF16),
            pltpu.VMEM((KEYS, PAIR), F32),
            pltpu.VMEM((KEYS, PAIR), F32),
            pltpu.VMEM((SPAN // HEAD, HEAD), jnp.int32),
        ],
        compiler_params=pltpu.CompilerParams(vmem_limit_bytes=48 << 20),
        name="attention_rows",
    )(docs, docs.reshape(-1, HEAD), kv, qg)


def scatter_kernel(rows_total, og, dkv, o0, o1, o2, o3, far, near, send_sem, recv_sem, down_send, down_recv, local_sem):
    base, spot, plane = place()
    above = (lax.rem(base + ROW, rows_total) + spot, plane)
    below = (lax.rem(base + rows_total - ROW, rows_total) + spot, plane)
    bar = pltpu.get_barrier_semaphore()
    for i in range(1, ROW):
        peer = (base + lax.rem(spot + i, ROW), plane)
        pl.semaphore_signal(bar, inc=1, device_id=peer, device_id_type=MESH)
    pl.semaphore_signal(bar, inc=1, device_id=above, device_id_type=MESH)
    pl.semaphore_signal(bar, inc=1, device_id=below, device_id_type=MESH)
    pl.semaphore_wait(bar, ROW + 1)

    downs = []
    locals_ = []
    for t in range(2):
        down = pltpu.make_async_remote_copy(
            src_ref=dkv.at[t, pl.ds(0, HALO), :],
            dst_ref=far.at[t],
            send_sem=down_send.at[t],
            recv_sem=down_recv.at[t],
            device_id=below,
            device_id_type=MESH,
        )
        down.start()
        downs.append(down)
        copy = pltpu.make_async_copy(dkv.at[t, pl.ds(2 * HALO, HALO), :], near.at[t], local_sem.at[t])
        copy.start()
        locals_.append(copy)

    outs = (o0, o1, o2, o3)
    columns = pl.ds(pl.multiple_of(spot * PAIR, PAIR), PAIR)

    def send(src, t, i, other):
        dst = outs[t].at[:, columns]
        if i == 0:
            pltpu.make_async_copy(src, dst, recv_sem.at[t]).start()
        else:
            pltpu.make_async_remote_copy(
                src_ref=src,
                dst_ref=dst,
                send_sem=send_sem.at[t],
                recv_sem=recv_sem.at[t],
                device_id=(base + other, plane),
                device_id_type=MESH,
            ).start()

    def rows(offset):
        return pl.ds(pl.multiple_of(offset, TOK), TOK)

    for t in range(2):
        for i in range(ROW):
            other = lax.rem(spot + i, ROW)
            send(og.at[t, rows(other * TOK), :], t, i, other)
    for t in range(2):
        for i in range(ROW):
            other = lax.rem(spot + i, ROW)

            @pl.when(other < 4)
            def _():
                send(dkv.at[t, rows(HALO + other * TOK), :], 2 + t, i, other)

    for t in range(2):
        locals_[t].wait()
        downs[t].wait()
        for b in range(4):
            span = pl.ds(b * TOK, TOK)
            near[t, span, :] = (near[t, span, :].astype(F32) + far[t, span, :].astype(F32)).astype(BF16)
        for i in range(ROW):
            other = lax.rem(spot + i, ROW)

            @pl.when(other >= 4)
            def _():
                send(near.at[t, rows((other - 4) * TOK), :], 2 + t, i, other)

    for t in range(4):
        wait_bytes(outs[t], recv_sem.at[t])
        wait_bytes(og.at[0, pl.ds(0, (ROW - 1) * TOK), :], send_sem.at[t])


def scatter_outputs(rows_total, og, dkv):
    any_space = pl.BlockSpec(memory_space=pl.ANY)
    return pl.pallas_call(
        functools.partial(scatter_kernel, rows_total),
        out_shape=tuple(jax.ShapeDtypeStruct((TOK, ROW * PAIR), BF16) for _ in range(4)),
        in_specs=[any_space] * 2,
        out_specs=(any_space,) * 4,
        scratch_shapes=[
            pltpu.VMEM((2, HALO, PAIR), BF16),
            pltpu.VMEM((2, HALO, PAIR), BF16),
            pltpu.SemaphoreType.DMA((4,)),
            pltpu.SemaphoreType.DMA((4,)),
            pltpu.SemaphoreType.DMA((2,)),
            pltpu.SemaphoreType.DMA((2,)),
            pltpu.SemaphoreType.DMA((2,)),
        ],
        compiler_params=pltpu.CompilerParams(collective_id=1, has_side_effects=True),
        name="scatter_outputs",
    )(og, dkv)


def solution(mesh):
    rows_total = mesh.shape["seq"]

    def on_device(doc_ids, attn_queries, attn_keys, attn_values, attn_cot):
        kv, qg = gather_inputs(rows_total, attn_queries, attn_keys, attn_values, attn_cot)
        og, dkv = attention(doc_ids, kv, qg)
        attn_out, query_grad, key_grad, value_grad = scatter_outputs(rows_total, og, dkv)
        return attn_out, query_grad, key_grad, value_grad

    tokens = P(("seq", "chan"), None)
    return jax.shard_map(
        on_device,
        mesh=mesh,
        in_specs=(P(), tokens, tokens, tokens, tokens),
        out_specs=(P("seq", "chan"),) * 4,
        check_vma=False,
    )
```

time: 358 us -> 152 us (0.42)
  waiting for transfers between devices: 157 us -> 0 us
  Pallas kernels: 0 us -> 141 us
  matrix products: 77.3 us -> 0 us
  starting transfers between devices: 66.1 us -> 0 us
  other arithmetic: 27.3 us -> 0 us
  local copies, waits for them, and re-layouts: 26.2 us -> 9.64 us
    pallas_call x0 -> x3, Pallas kernels: none -> 141 us  [the longest x1 58.1 us: scatter_outputs(): pl.pallas_call(functools.partial(scatter_kernel, rows_total), out_shape=t...]
    ppermute x16 -> x0, waiting for transfers between devices: 128 us -> none  [shifted(): return lax.ppermute(value, axis, pairs)]
    dot_general x30 -> x0, matrix products: 77.3 us -> none  [the longest x5 33.2 us: weight_grads(): jnp.einsum('qhe,khe->hqk', cot_heads, value_block, preferred_element_type...]
    ppermute x16 -> x0, starting transfers between devices: 48.8 us -> none  [shifted(): return lax.ppermute(value, axis, pairs)]
    all_to_all x4 -> x0, waiting for transfers between devices: 29.3 us -> none  [the longest x1 13.1 us: attention_layer(): lax.all_to_all(attn_keys, 'chan', split_axis=1, concat_axis=0, tiled=True)]
    all_to_all x4 -> x0, starting transfers between devices: 17.4 us -> none  [the longest x1 5.86 us: attention_layer(): lax.all_to_all(attn_keys, 'chan', split_axis=1, concat_axis=0, tiled=True)]
    convert_element_type x3 -> x0, other arithmetic: 17 us -> none  [the longest x1 13.2 us: attention_layer(): (weights[offset].astype(jnp.float32) * (dweights[offset] - rowdot[..., No...]
    all_to_all x4 -> x0, local copies, waits for them, and re-layouts: 6.77 us -> none  [the longest x1 2.39 us: attention_layer(): lax.all_to_all(attn_keys, 'chan', split_axis=1, concat_axis=0, tiled=True)]
  transfers between devices with their start and end apart: 20 -> 0, of which waited for: 17 -> 0; matrix products, arithmetic and copies ran while one was open for 28% -> 0% of each run, Pallas kernels for 0% -> 0%
where the time goes in v1:
time: 152 us; the launch traced here: 151 us
  Pallas kernels  141 us (93%)
  local copies, waits for them, and re-layouts  9.64 us (6%)
    pallas_call x1, Pallas kernels, scatter_outputs(): pl.pallas_call(functools.partial(scatter_kernel, rows_total), out_shape=t...  58.1 us
    pallas_call x1, Pallas kernels, gather_inputs(): pl.pallas_call(functools.partial(gather_kernel, rows_total), out_shape=(j...  56.6 us
    pallas_call x1, Pallas kernels, attention(): pl.pallas_call(attention_kernel, out_shape=(jax.ShapeDtypeStruct((2, SPAN...  26.3 us
    unnamed x14, local copies, waits for them, and re-layouts  9.64 us

profile of v1, /device:TPU:1, one launch (start us, length us, event | category | flops | bytes accessed | tf_op | source)
XLA Modules:
  0.0 151.4 jit_solution(6340108261816643726)
XLA Ops:
  0.6 0.0 copy-start.2
  0.6 56.6 %gather_inputs.1 = (bf16[2,3072,256]{2,1,0:T(8,128)(2,1)}, bf16[2,2048,256]{2,1,0:T(8,128)(2,1)}) custom-call(bf16[64,8192]{1,0:T(8,128)(2,1)} %q.1, bf16[64,8192]{1,0:T(8,128)(2,1)} %k.1, bf16[64,8192]{1,0:T(8,128)(2,1)} %v.1, bf16[64,8192]{1,0:T(8,128)(2,1)} %g.1), custom_call_target="tpu_custom_call" | custom-call | tf_op jit(solution)/shard_map/gather_inputs/pallas_call | solution.py:107
  57.3 0.0 copy-done.2
  57.3 0.0 copy-start.1
  57.3 1.6 %copy-done.1 = bf16[2,2048,256]{2,1,0:T(8,128)(2,1)S(1)} copy-done((bf16[2,2048,256]{2,1,0:T(8,128)(2,1)S(1)}, bf16[2,2048,256]{2,1,0:T(8,128)(2,1)}, u32[]{:S(2)}) %copy-start.1) | copy-done | bytes 2097176
  58.9 26.3 %attention_rows.1 = (bf16[2,2048,256]{2,1,0:T(8,128)(2,1)S(1)}, bf16[2,3072,256]{2,1,0:T(8,128)(2,1)}) custom-call(s32[8192]{0:T(1024)S(1)} %copy-done.2, s32[64,128]{1,0:T(8,128)S(1)} %bitcast.1, bf16[2,3072,256]{2,1,0:T(8,128)(2,1)} %get-tuple-element.8.kv, bf16[2,2048,256]{2,1,0:T(8,128)(2,1)S(1)} %copy-done.1), custom_call_target="tpu_custom_call" | custom-call | tf_op jit(solution)/shard_map/attention_rows/pallas_call | solution.py:245
  85.2 0.0 copy-start
  85.2 1.3 copy-done
  86.6 58.1 %scatter_outputs.1 = (bf16[256,2048]{1,0:T(8,128)(2,1)}, bf16[256,2048]{1,0:T(8,128)(2,1)}, bf16[256,2048]{1,0:T(8,128)(2,1)}, bf16[256,2048]{1,0:T(8,128)(2,1)}) custom-call(bf16[2,2048,256]{2,1,0:T(8,128)(2,1)} %copy-done, bf16[2,3072,256]{2,1,0:T(8,128)(2,1)} %get-tuple-element.11.dkv), custom_call_target="tpu_custom_call" | custom-call | tf_op jit(solution)/shard_map/scatter_outputs/pallas_call | solution.py:348
  144.7 0.0 copy-start.4
  144.7 0.0 copy-start.3
  144.7 2.5 %copy.13 = bf16[256,2048]{1,0:T(8,128)(2,1)} copy(bf16[256,2048]{1,0:T(8,128)(2,1)} %get-tuple-element.16) | data formatting | bytes 2097152
  147.2 2.3 %copy.14 = bf16[256,2048]{1,0:T(8,128)(2,1)} copy(bf16[256,2048]{1,0:T(8,128)(2,1)} %get-tuple-element.17) | data formatting | bytes 2097152
  149.5 0.0 copy-done.4
  149.5 1.0 copy.15
  150.4 0.0 copy-done.3
  150.4 1.0 copy.16
Async XLA Ops:
  0.6 56.7 %copy-start.2 = (s32[8192]{0:T(1024)S(1)}, s32[8192]{0:T(1024)}, u32[]{:S(2)}) copy-start(s32[8192]{0:T(1024)} %docs_s.1) | copy-start | bytes 98308
  57.3 1.6 %copy-start.1 = (bf16[2,2048,256]{2,1,0:T(8,128)(2,1)S(1)}, bf16[2,2048,256]{2,1,0:T(8,128)(2,1)}, u32[]{:S(2)}) copy-start(bf16[2,2048,256]{2,1,0:T(8,128)(2,1)} %get-tuple-element.9.qg) | copy-start | bytes 6291460
  85.2 1.3 copy-start
  144.7 4.8 %copy-start.4 = (bf16[256,2048]{1,0:T(8,128)(2,1)S(1)}, bf16[256,2048]{1,0:T(8,128)(2,1)}, u32[]{:S(2)}) copy-start(bf16[256,2048]{1,0:T(8,128)(2,1)} %get-tuple-element.18) | copy-start | bytes 3145732
  144.7 5.7 %copy-start.3 = (bf16[256,2048]{1,0:T(8,128)(2,1)S(1)}, bf16[256,2048]{1,0:T(8,128)(2,1)}, u32[]{:S(2)}) copy-start(bf16[256,2048]{1,0:T(8,128)(2,1)} %get-tuple-element.19) | copy-start | bytes 3145732

commit v2 on v0

v2 whole, which is shorter than its diff:
```python
import functools

import jax
import jax.numpy as jnp
from jax import lax
from jax.experimental import pallas as pl
from jax.experimental.pallas import tpu as pltpu
from jax.sharding import PartitionSpec as P

MESH = pl.DeviceIdType.MESH
HEAD = 128
ROW = 8
CHAN = 4
TOK = 256
PIECE = 64
SPAN = ROW * TOK
HALO = 1024
KEYS = SPAN + HALO
PAIR = 2 * HEAD
LOG2E = 1.4426950408889634
NEG = -1e30
F32 = jnp.float32
BF16 = jnp.bfloat16
DOCS = 16


def place():
    shard = lax.axis_index("seq")
    plane = lax.axis_index("chan")
    spot = lax.rem(shard, ROW)
    return shard - spot, spot, plane


def wait_bytes(ref, sem):
    pltpu.make_async_copy(ref, ref, sem).wait()


def dot(a, b):
    return jnp.dot(a, b, preferred_element_type=F32)


def whole_kernel(
    rows_total, q, k, v, g, docs, land,
    kv, qg, og, dkv, far, scores, weights, keys_t, values_t, dk_acc, dv_acc, limits,
    send_sem, recv_sem, up_send, up_recv, down_send, down_recv, home_send, home_recv,
):
    base, spot, plane = place()
    half = spot // 4
    above = (lax.rem(base + ROW, rows_total) + spot, plane)
    below = (lax.rem(base + rows_total - ROW, rows_total) + spot, plane)
    scale = HEAD ** -0.5
    log_scale = scale * LOG2E

    bar = pltpu.get_barrier_semaphore()
    for i in range(ROW):
        for j in range(CHAN):
            if i or j:
                peer = (base + lax.rem(spot + i, ROW), lax.rem(plane + j, CHAN))
                pl.semaphore_signal(bar, inc=1, device_id=peer, device_id_type=MESH)
    pl.semaphore_signal(bar, inc=1, device_id=above, device_id_type=MESH)
    pl.semaphore_signal(bar, inc=1, device_id=below, device_id_type=MESH)
    pl.semaphore_wait(bar, ROW * CHAN + 1)

    def send(src, t, h):
        offset = spot * TOK + plane * PIECE + (HALO if t < 2 else 0)
        rows = pl.ds(pl.multiple_of(offset, PIECE), PIECE)
        dst = (kv if t < 2 else qg).at[t % 2, h, rows, :]
        arrival = recv_sem.at[t, h, half]

        def columns(room, floor):
            first = (floor * ROW + room) * PAIR + h * HEAD
            return pl.ds(pl.multiple_of(first, HEAD), HEAD)

        pltpu.make_async_copy(src.at[:, columns(spot, plane)], dst, arrival).start()

        def one(n, carry):
            room = lax.rem(spot + n // CHAN, ROW)
            floor = lax.rem(plane + lax.rem(n, CHAN), CHAN)
            pltpu.make_async_remote_copy(
                src_ref=src.at[:, columns(room, floor)],
                dst_ref=dst,
                send_sem=send_sem.at[t, h],
                recv_sem=arrival,
                device_id=(base + room, floor),
                device_id_type=MESH,
            ).start()
            return carry

        lax.fori_loop(1, ROW * CHAN, one, 0)

    def climb(t, h):
        return pltpu.make_async_remote_copy(
            src_ref=kv.at[t, h, pl.ds(2 * HALO, HALO), :],
            dst_ref=kv.at[t, h, pl.ds(0, HALO), :],
            send_sem=up_send.at[t, h],
            recv_sem=up_recv.at[t, h],
            device_id=above,
            device_id_type=MESH,
        )

    def raise_half(t, h):
        wait_bytes(kv.at[t, h, pl.ds(2 * HALO, HALO), :], recv_sem.at[t, h, 1])
        climb(t, h).start()

    def arrive(h):
        for t in range(2):
            wait_bytes(kv.at[t, h, pl.ds(HALO, HALO), :], recv_sem.at[t, h, 0])
            wait_bytes(qg.at[t, h, pl.ds(0, HALO), :], recv_sem.at[2 + t, h, 0])
            wait_bytes(qg.at[t, h, pl.ds(HALO, HALO), :], recv_sem.at[2 + t, h, 1])
        for t in range(2):
            climb(t, h).wait_recv()

    def drop(t, h):
        return pltpu.make_async_remote_copy(
            src_ref=dkv.at[t, h, pl.ds(0, HALO), :],
            dst_ref=far.at[t, h],
            send_sem=down_send.at[t, h],
            recv_sem=down_recv.at[t, h],
            device_id=below,
            device_id_type=MESH,
        )

    def go_home(src, t, h, i):
        other = lax.rem(spot + i, ROW)
        dst = land.at[t, h, spot]
        if i == 0:
            pltpu.make_async_copy(src, dst, home_recv.at[t, h]).start()
        else:
            pltpu.make_async_remote_copy(
                src_ref=src,
                dst_ref=dst,
                send_sem=home_send.at[t, h],
                recv_sem=home_recv.at[t, h],
                device_id=(base + other, plane),
                device_id_type=MESH,
            ).start()

    def rows_at(offset):
        return pl.ds(pl.multiple_of(offset, TOK), TOK)

    def home_queries(h):
        for t in range(2):
            for i in range(ROW):
                go_home(og.at[t, h, rows_at(lax.rem(spot + i, ROW) * TOK), :], t, h, i)

    def home_keys(h, upper):
        for t in range(2):
            for i in range(ROW):
                other = lax.rem(spot + i, ROW)

                @pl.when((other >= 4) if upper else (other < 4))
                def _():
                    go_home(dkv.at[t, h, rows_at(HALO + other * TOK), :], 2 + t, h, i)

    def set_limits():
        all_docs = docs[...]
        own = docs[pl.ds(pl.multiple_of(base * (TOK // HEAD), 16), SPAN // HEAD), :]
        starts = jnp.zeros_like(own)
        for d in range(1, DOCS):
            below_d = jnp.where(all_docs < d, 1.0, 0.0)
            count = jnp.sum(jnp.sum(below_d, axis=0, keepdims=True), axis=1, keepdims=True)
            starts = jnp.where(own == d, jnp.broadcast_to(count.astype(jnp.int32), own.shape), starts)
        limits[...] = starts - (base * TOK - HALO)

    key_iota = lax.broadcasted_iota(jnp.int32, (TOK, TOK), 0)
    diagonal = key_iota <= lax.broadcasted_iota(jnp.int32, (TOK, TOK), 1)
    reach = HALO // TOK + 1

    def prepare(h):
        for b in range(KEYS // TOK):
            span = pl.ds(b * TOK, TOK)
            keys_t[:, span] = kv[0, h, span, :].T
            values_t[:, span] = kv[1, h, span, :].T
        dk_acc[...] = jnp.zeros_like(dk_acc)
        dv_acc[...] = jnp.zeros_like(dv_acc)

    def attend(h, first, last):
        def one_block(b, carry):
            rows = rows_at(b * TOK)
            low = jnp.concatenate([limits[pl.ds(2 * b, 1), :], limits[pl.ds(2 * b + 1, 1), :]], axis=1)
            queries = qg[0, h, rows, :]
            queries_t = queries.T
            cot_raw_t = qg[1, h, rows, :].T

            def key_rows(o):
                return rows_at((b + reach - 1 - o) * TOK)

            peak = jnp.full((1, TOK), NEG, F32)
            for o in range(reach):
                raw = dot(kv[0, h, key_rows(o), :], queries_t)
                inside = key_iota >= low - (b + reach - 1 - o) * TOK
                if o == 0:
                    inside = inside & diagonal
                raw = jnp.where(inside, raw, NEG)
                scores[o] = raw
                peak = jnp.maximum(peak, jnp.max(raw, axis=0, keepdims=True))
            shift = peak * log_scale
            total = jnp.zeros((1, TOK), F32)
            mixed = jnp.zeros((HEAD, TOK), F32)
            for o in range(reach):
                expo = jnp.exp2(scores[o] * log_scale - shift)
                small = expo.astype(BF16)
                weights[o] = small
                total = total + jnp.sum(expo, axis=0, keepdims=True)
                mixed = mixed + dot(values_t[:, key_rows(o)], small)
            inverse = 1.0 / total
            mixed = mixed * inverse
            og[0, h, rows, :] = mixed.T.astype(BF16)
            cot_t = (cot_raw_t.astype(F32) * inverse).astype(BF16)
            rowdot = jnp.sum(cot_t.astype(F32) * mixed, axis=0, keepdims=True)
            cot = cot_t.T
            grad = jnp.zeros((HEAD, TOK), F32)
            for o in range(reach):
                keys = key_rows(o)
                weight = weights[o]
                dweight = dot(kv[1, h, keys, :], cot_t)
                dscore = (weight.astype(F32) * (dweight - rowdot)).astype(BF16)
                dv_acc[keys, :] += dot(weight, cot)
                dk_acc[keys, :] += dot(dscore, queries)
                grad = grad + dot(keys_t[:, keys], dscore)
            og[1, h, rows, :] = (grad * scale).T.astype(BF16)
            return carry

        lax.fori_loop(first, last, one_block, 0)

    def settle(h, first, last):
        for b in range(first, last):
            span = pl.ds(b * TOK, TOK)
            dkv[0, h, span, :] = (dk_acc[span, :] * scale).astype(BF16)
            dkv[1, h, span, :] = dv_acc[span, :].astype(BF16)

    def join(h):
        for t in range(2):
            drop(t, h).wait_recv()
            for b in range(4):
                span = pl.ds(2 * HALO + b * TOK, TOK)
                near = dkv[t, h, span, :].astype(F32)
                dkv[t, h, span, :] = (near + far[t, h, pl.ds(b * TOK, TOK), :].astype(F32)).astype(BF16)
        home_keys(h, True)

    send(k, 0, 0)
    send(v, 1, 0)
    set_limits()
    raise_half(0, 0)
    send(q, 2, 0)
    raise_half(1, 0)
    send(g, 3, 0)
    send(k, 0, 1)
    send(v, 1, 1)
    send(q, 2, 1)
    send(g, 3, 1)
    arrive(0)
    prepare(0)
    attend(0, 0, 4)
    raise_half(0, 1)
    settle(0, 0, 4)
    for t in range(2):
        drop(t, 0).start()
    attend(0, 4, 8)
    raise_half(1, 1)
    settle(0, 4, 12)
    home_queries(0)
    home_keys(0, False)
    arrive(1)
    prepare(1)
    attend(1, 0, 4)
    settle(1, 0, 4)
    for t in range(2):
        drop(t, 1).start()
    join(0)
    attend(1, 4, 8)
    settle(1, 4, 12)
    home_queries(1)
    home_keys(1, False)
    join(1)

    for h in range(2):
        for t in range(2):
            climb(t, h).wait_send()
            drop(t, h).wait_send()
        for t in range(4):
            wait_bytes(qg.at[0, 0, pl.ds(0, (ROW * CHAN - 1) * PIECE), :], send_sem.at[t, h])
            wait_bytes(og.at[0, 0, pl.ds(0, (ROW - 1) * TOK), :], home_send.at[t, h])
            wait_bytes(land.at[t, h], home_recv.at[t, h])


def whole(rows_total, docs, q, k, v, g):
    any_space = pl.BlockSpec(memory_space=pl.ANY)
    vmem = pl.BlockSpec(memory_space=pltpu.VMEM)
    dma = pltpu.SemaphoreType.DMA
    return pl.pallas_call(
        functools.partial(whole_kernel, rows_total),
        out_shape=jax.ShapeDtypeStruct((4, 2, ROW, TOK, HEAD), BF16),
        in_specs=[pl.BlockSpec(memory_space=pltpu.MemorySpace.HBM)] * 4 + [vmem],
        out_specs=pl.BlockSpec(memory_space=pltpu.MemorySpace.HBM),
        scratch_shapes=[
            pltpu.VMEM((2, 2, KEYS, HEAD), BF16),
            pltpu.VMEM((2, 2, SPAN, HEAD), BF16),
            pltpu.VMEM((2, 2, SPAN, HEAD), BF16),
            pltpu.VMEM((2, 2, KEYS, HEAD), BF16),
            pltpu.VMEM((2, 2, HALO, HEAD), BF16),
            pltpu.VMEM((5, TOK, TOK), F32),
            pltpu.VMEM((5, TOK, TOK), BF16),
            pltpu.VMEM((HEAD, KEYS), BF16),
            pltpu.VMEM((HEAD, KEYS), BF16),
            pltpu.VMEM((KEYS, HEAD), F32),
            pltpu.VMEM((KEYS, HEAD), F32),
            pltpu.VMEM((SPAN // HEAD, HEAD), jnp.int32),
            dma((4, 2)),
            dma((4, 2, 2)),
            dma((2, 2)),
            dma((2, 2)),
            dma((2, 2)),
            dma((2, 2)),
            dma((4, 2)),
            dma((4, 2)),
        ],
        compiler_params=pltpu.CompilerParams(
            collective_id=0, has_side_effects=True, vmem_limit_bytes=60 << 20
        ),
        name="whole_rows",
    )(q, k, v, g, docs.reshape(-1, HEAD))


def lay_kernel(land, o0, o1, o2, o3, sems):
    copies = []
    for t, out in enumerate((o0, o1, o2, o3)):
        for h in range(2):
            for r in range(ROW):
                lanes = pl.ds((2 * r + h) * HEAD, HEAD)
                copies.append(pltpu.make_async_copy(land.at[t, h, r], out.at[:, lanes], sems.at[t, h, r]))
    for copy in copies:
        copy.start()
    for copy in copies:
        copy.wait()


def lay_out(land):
    any_space = pl.BlockSpec(memory_space=pl.ANY)
    return pl.pallas_call(
        lay_kernel,
        out_shape=tuple(jax.ShapeDtypeStruct((TOK, ROW * PAIR), BF16) for _ in range(4)),
        in_specs=[pl.BlockSpec(memory_space=pltpu.MemorySpace.HBM)],
        out_specs=(any_space,) * 4,
        scratch_shapes=[pltpu.SemaphoreType.DMA((4, 2, ROW))],
        name="lay_out",
    )(land)


def solution(mesh):
    rows_total = mesh.shape["seq"]

    def on_device(doc_ids, attn_queries, attn_keys, attn_values, attn_cot):
        land = whole(rows_total, doc_ids, attn_queries, attn_keys, attn_values, attn_cot)
        return lay_out(land)

    tokens = P(("seq", "chan"), None)
    return jax.shard_map(
        on_device,
        mesh=mesh,
        in_specs=(P(), tokens, tokens, tokens, tokens),
        out_specs=(P("seq", "chan"),) * 4,
        check_vma=False,
    )
```

time: 358 us -> 232 us (0.65)
  Pallas kernels: 0 us -> 231 us
  waiting for transfers between devices: 157 us -> 0 us
  matrix products: 77.3 us -> 0 us
  starting transfers between devices: 66.1 us -> 0 us
  other arithmetic: 27.3 us -> 0 us
  local copies, waits for them, and re-layouts: 26.2 us -> 0 us
    pallas_call x0 -> x2, Pallas kernels: none -> 231 us  [the longest x1 129 us: lay_out(): pl.pallas_call(lay_kernel, out_shape=tuple((jax.ShapeDtypeStruct((TOK, RO...]
    ppermute x16 -> x0, waiting for transfers between devices: 128 us -> none  [shifted(): return lax.ppermute(value, axis, pairs)]
    dot_general x30 -> x0, matrix products: 77.3 us -> none  [the longest x5 33.2 us: weight_grads(): jnp.einsum('qhe,khe->hqk', cot_heads, value_block, preferred_element_type...]
    ppermute x16 -> x0, starting transfers between devices: 48.8 us -> none  [shifted(): return lax.ppermute(value, axis, pairs)]
    all_to_all x4 -> x0, waiting for transfers between devices: 29.3 us -> none  [the longest x1 13.1 us: attention_layer(): lax.all_to_all(attn_keys, 'chan', split_axis=1, concat_axis=0, tiled=True)]
    all_to_all x4 -> x0, starting transfers between devices: 17.4 us -> none  [the longest x1 5.86 us: attention_layer(): lax.all_to_all(attn_keys, 'chan', split_axis=1, concat_axis=0, tiled=True)]
    convert_element_type x3 -> x0, other arithmetic: 17 us -> none  [the longest x1 13.2 us: attention_layer(): (weights[offset].astype(jnp.float32) * (dweights[offset] - rowdot[..., No...]
    unnamed x68 -> x0, local copies, waits for them, and re-layouts: 12 us -> none
  transfers between devices with their start and end apart: 20 -> 0, of which waited for: 17 -> 0; matrix products, arithmetic and copies ran while one was open for 28% -> 0% of each run, Pallas kernels for 0% -> 0%
where the time goes in v2:
time: 232 us; the launch traced here: 231 us
  Pallas kernels  231 us (100%)
    pallas_call x1, Pallas kernels, lay_out(): pl.pallas_call(lay_kernel, out_shape=tuple((jax.ShapeDtypeStruct((TOK, RO...  129 us
    pallas_call x1, Pallas kernels, whole(): pl.pallas_call(functools.partial(whole_kernel, rows_total), out_shape=jax...  102 us

profile of v2, /device:TPU:1, one launch (start us, length us, event | category | flops | bytes accessed | tf_op | source)
XLA Modules:
  0.0 231.5 jit_solution(11084142737838121172)
XLA Ops:
  0.6 102.1 %whole_rows.1.land = bf16[4,2,8,256,128]{4,3,2,1,0:T(8,128)(2,1)} custom-call(bf16[64,8192]{1,0:T(8,128)(2,1)} %q.1, bf16[64,8192]{1,0:T(8,128)(2,1)} %k.1, bf16[64,8192]{1,0:T(8,128)(2,1)} %v.1, bf16[64,8192]{1,0:T(8,128)(2,1)} %g.1, s32[64,128]{1,0:T(8,128)} %bitcast.1), custom_call_target="tpu_custom_call" | custom-call | tf_op jit(solution)/shard_map/whole_rows/pallas_call | solution.py:291
  102.8 128.7 %lay_out.1 = (bf16[256,2048]{1,0:T(8,128)(2,1)}, bf16[256,2048]{1,0:T(8,128)(2,1)}, bf16[256,2048]{1,0:T(8,128)(2,1)}, bf16[256,2048]{1,0:T(8,128)(2,1)}) custom-call(bf16[4,2,8,256,128]{4,3,2,1,0:T(8,128)(2,1)} %whole_rows.1.land), custom_call_target="tpu_custom_call" | custom-call | tf_op jit(solution)/shard_map/lay_out/pallas_call | solution.py:340

commit v3 on v2

--- a/solution.py
+++ b/solution.py
@@ -322,27 +322,20 @@
     )(q, k, v, g, docs.reshape(-1, HEAD))
 
 
-def lay_kernel(land, o0, o1, o2, o3, sems):
-    copies = []
+def lay_kernel(land, o0, o1, o2, o3):
     for t, out in enumerate((o0, o1, o2, o3)):
-        for h in range(2):
-            for r in range(ROW):
-                lanes = pl.ds((2 * r + h) * HEAD, HEAD)
-                copies.append(pltpu.make_async_copy(land.at[t, h, r], out.at[:, lanes], sems.at[t, h, r]))
-    for copy in copies:
-        copy.start()
-    for copy in copies:
-        copy.wait()
+        for r in range(2):
+            for h in range(2):
+                out[:, pl.ds((2 * r + h) * HEAD, HEAD)] = land[t, h, r]
 
 
 def lay_out(land):
-    any_space = pl.BlockSpec(memory_space=pl.ANY)
     return pl.pallas_call(
         lay_kernel,
+        grid=(ROW // 2,),
         out_shape=tuple(jax.ShapeDtypeStruct((TOK, ROW * PAIR), BF16) for _ in range(4)),
-        in_specs=[pl.BlockSpec(memory_space=pltpu.MemorySpace.HBM)],
-        out_specs=(any_space,) * 4,
-        scratch_shapes=[pltpu.SemaphoreType.DMA((4, 2, ROW))],
+        in_specs=[pl.BlockSpec((4, 2, 2, TOK, HEAD), lambda r: (0, 0, r, 0, 0))],
+        out_specs=tuple(pl.BlockSpec((TOK, 2 * PAIR), lambda r: (0, r)) for _ in range(4)),
         name="lay_out",
     )(land)
 

time: 232 us -> 108 us (0.47)
  Pallas kernels: 231 us -> 107 us
    pallas_call x1, Pallas kernels: 129 us -> 4.94 us  [lay_out(): pl.pallas_call(lay_kernel, grid=(ROW // 2,), out_shape=tuple((jax.ShapeDt...]
where the time goes in v3:
time: 108 us
  Pallas kernels  107 us (99%)
    pallas_call x1, Pallas kernels, whole(): pl.pallas_call(functools.partial(whole_kernel, rows_total), out_shape=jax...  102 us
    pallas_call x1, Pallas kernels, lay_out(): pl.pallas_call(lay_kernel, grid=(ROW // 2,), out_shape=tuple((jax.ShapeDt...  4.94 us

profile of v3, /device:TPU:1, one launch (start us, length us, event | category | flops | bytes accessed | tf_op | source)
XLA Modules:
  0.0 107.7 jit_solution(14064816386589204912)
XLA Ops:
  0.6 102.1 %whole_rows.1.land = bf16[4,2,8,256,128]{4,3,2,1,0:T(8,128)(2,1)} custom-call(bf16[64,8192]{1,0:T(8,128)(2,1)} %q.1, bf16[64,8192]{1,0:T(8,128)(2,1)} %k.1, bf16[64,8192]{1,0:T(8,128)(2,1)} %v.1, bf16[64,8192]{1,0:T(8,128)(2,1)} %g.1, s32[64,128]{1,0:T(8,128)} %bitcast.1), custom_call_target="tpu_custom_call" | custom-call | tf_op jit(solution)/shard_map/whole_rows/pallas_call | solution.py:291
  102.8 4.9 %lay_out.1 = (bf16[256,2048]{1,0:T(8,128)(2,1)}, bf16[256,2048]{1,0:T(8,128)(2,1)}, bf16[256,2048]{1,0:T(8,128)(2,1)}, bf16[256,2048]{1,0:T(8,128)(2,1)}) custom-call(bf16[4,2,8,256,128]{4,3,2,1,0:T(8,128)(2,1)} %whole_rows.1.land), custom_call_target="tpu_custom_call" | custom-call | tf_op jit(solution)/shard_map/lay_out/pallas_call | solution.py:333

commit v4 on v2

--- a/solution.py
+++ b/solution.py
@@ -40,9 +40,9 @@
 
 
 def whole_kernel(
-    rows_total, q, k, v, g, docs, land,
-    kv, qg, og, dkv, far, scores, weights, keys_t, values_t, dk_acc, dv_acc, limits,
-    send_sem, recv_sem, up_send, up_recv, down_send, down_recv, home_send, home_recv,
+    rows_total, q, k, v, g, docs_far, land,
+    docs, kv, qg, og, dkv, far, scores, weights, keys_t, values_t, dk_acc, dv_acc, limits,
+    send_sem, recv_sem, up_send, up_recv, down_send, down_recv, home_send, home_recv, docs_sem,
 ):
     base, spot, plane = place()
     half = spot // 4
@@ -51,6 +51,8 @@
     scale = HEAD ** -0.5
     log_scale = scale * LOG2E
 
+    fetch = pltpu.make_async_copy(docs_far, docs, docs_sem)
+    fetch.start()
     bar = pltpu.get_barrier_semaphore()
     for i in range(ROW):
         for j in range(CHAN):
@@ -143,14 +145,10 @@
             for i in range(ROW):
                 go_home(og.at[t, h, rows_at(lax.rem(spot + i, ROW) * TOK), :], t, h, i)
 
-    def home_keys(h, upper):
+    def home_keys(h):
         for t in range(2):
             for i in range(ROW):
-                other = lax.rem(spot + i, ROW)
-
-                @pl.when((other >= 4) if upper else (other < 4))
-                def _():
-                    go_home(dkv.at[t, h, rows_at(HALO + other * TOK), :], 2 + t, h, i)
+                go_home(dkv.at[t, h, rows_at(HALO + lax.rem(spot + i, ROW) * TOK), :], 2 + t, h, i)
 
     def set_limits():
         all_docs = docs[...]
@@ -236,10 +234,11 @@
                 span = pl.ds(2 * HALO + b * TOK, TOK)
                 near = dkv[t, h, span, :].astype(F32)
                 dkv[t, h, span, :] = (near + far[t, h, pl.ds(b * TOK, TOK), :].astype(F32)).astype(BF16)
-        home_keys(h, True)
+        home_keys(h)
 
     send(k, 0, 0)
     send(v, 1, 0)
+    fetch.wait()
     set_limits()
     raise_half(0, 0)
     send(q, 2, 0)
@@ -260,18 +259,16 @@
     raise_half(1, 1)
     settle(0, 4, 12)
     home_queries(0)
-    home_keys(0, False)
     arrive(1)
+    join(0)
     prepare(1)
     attend(1, 0, 4)
     settle(1, 0, 4)
     for t in range(2):
         drop(t, 1).start()
-    join(0)
     attend(1, 4, 8)
     settle(1, 4, 12)
     home_queries(1)
-    home_keys(1, False)
     join(1)
 
     for h in range(2):
@@ -291,9 +288,10 @@
     return pl.pallas_call(
         functools.partial(whole_kernel, rows_total),
         out_shape=jax.ShapeDtypeStruct((4, 2, ROW, TOK, HEAD), BF16),
-        in_specs=[pl.BlockSpec(memory_space=pltpu.MemorySpace.HBM)] * 4 + [vmem],
-        out_specs=pl.BlockSpec(memory_space=pltpu.MemorySpace.HBM),
+        in_specs=[pl.BlockSpec(memory_space=pltpu.MemorySpace.HBM)] * 5,
+        out_specs=pl.BlockSpec(memory_space=pltpu.MemorySpace.VMEM),
         scratch_shapes=[
+            pltpu.VMEM((docs.shape[0] // HEAD, HEAD), jnp.int32),
             pltpu.VMEM((2, 2, KEYS, HEAD), BF16),
             pltpu.VMEM((2, 2, SPAN, HEAD), BF16),
             pltpu.VMEM((2, 2, SPAN, HEAD), BF16),
@@ -314,35 +312,36 @@
             dma((2, 2)),
             dma((4, 2)),
             dma((4, 2)),
+            dma,
         ],
         compiler_params=pltpu.CompilerParams(
-            collective_id=0, has_side_effects=True, vmem_limit_bytes=60 << 20
+            collective_id=0, has_side_effects=True, vmem_limit_bytes=48 << 20
         ),
         name="whole_rows",
-    )(q, k, v, g, docs.reshape(-1, HEAD))
-
-
-def lay_kernel(land, o0, o1, o2, o3, sems):
-    copies = []
-    for t, out in enumerate((o0, o1, o2, o3)):
+    )(*[pltpu.with_memory_space_constraint(a, pltpu.MemorySpace.HBM) for a in (q, k, v, g, docs.reshape(-1, HEAD))])
+
+
+def lay_kernel(land, o0, o1, o2, o3, out_sem):
+    outs = (o0, o1, o2, o3)
+    for t in range(4):
         for h in range(2):
             for r in range(ROW):
                 lanes = pl.ds((2 * r + h) * HEAD, HEAD)
-                copies.append(pltpu.make_async_copy(land.at[t, h, r], out.at[:, lanes], sems.at[t, h, r]))
-    for copy in copies:
-        copy.start()
-    for copy in copies:
-        copy.wait()
+                pltpu.make_async_copy(land.at[t, h, r], outs[t].at[:, lanes], out_sem.at[t]).start()
+    for t in range(4):
+        pltpu.make_async_copy(outs[t], outs[t], out_sem.at[t]).wait()
 
 
 def lay_out(land):
     any_space = pl.BlockSpec(memory_space=pl.ANY)
+    land = pltpu.with_memory_space_constraint(land, pltpu.MemorySpace.VMEM)
     return pl.pallas_call(
         lay_kernel,
         out_shape=tuple(jax.ShapeDtypeStruct((TOK, ROW * PAIR), BF16) for _ in range(4)),
-        in_specs=[pl.BlockSpec(memory_space=pltpu.MemorySpace.HBM)],
+        in_specs=[pl.BlockSpec(memory_space=pltpu.MemorySpace.VMEM)],
         out_specs=(any_space,) * 4,
-        scratch_shapes=[pltpu.SemaphoreType.DMA((4, 2, ROW))],
+        scratch_shapes=[pltpu.SemaphoreType.DMA((4,))],
+        compiler_params=pltpu.CompilerParams(vmem_limit_bytes=8 << 20),
         name="lay_out",
     )(land)
 

time: 232 us -> 104 us (0.45)
  Pallas kernels: 231 us -> 103 us
    pallas_call x1, Pallas kernels: 129 us -> 2 us  [lay_out(): pl.pallas_call(lay_kernel, out_shape=tuple((jax.ShapeDtypeStruct((TOK, RO...]
where the time goes in v4:
time: 104 us
  Pallas kernels  103 us (99%)
    pallas_call x1, Pallas kernels, whole(): pl.pallas_call(functools.partial(whole_kernel, rows_total), out_shape=jax...  101 us

profile of v4, /device:TPU:1, one launch (start us, length us, event | category | flops | bytes accessed | tf_op | source)
XLA Modules:
  0.0 103.8 jit_solution(18140673005775556689)
XLA Ops:
  0.6 101.1 %whole_rows.1.land = bf16[4,2,8,256,128]{4,3,2,1,0:T(8,128)(2,1)S(1)} custom-call(bf16[64,8192]{1,0:T(8,128)(2,1)} %q.1, bf16[64,8192]{1,0:T(8,128)(2,1)} %k.1, bf16[64,8192]{1,0:T(8,128)(2,1)} %v.1, bf16[64,8192]{1,0:T(8,128)(2,1)} %g.1, s32[64,128]{1,0:T(8,128)} %bitcast.1), custom_call_target="tpu_custom_call" | custom-call | tf_op jit(solution)/shard_map/whole_rows/pallas_call | solution.py:288
  101.8 2.0 %lay_out.1 = (bf16[256,2048]{1,0:T(8,128)(2,1)}, bf16[256,2048]{1,0:T(8,128)(2,1)}, bf16[256,2048]{1,0:T(8,128)(2,1)}, bf16[256,2048]{1,0:T(8,128)(2,1)}) custom-call(bf16[4,2,8,256,128]{4,3,2,1,0:T(8,128)(2,1)S(1)} %whole_rows.1.land), custom_call_target="tpu_custom_call" | custom-call | tf_op jit(solution)/shard_map/lay_out/pallas_call | solution.py:338

commit v5 on v4

--- a/solution.py
+++ b/solution.py
@@ -54,13 +54,12 @@
     fetch = pltpu.make_async_copy(docs_far, docs, docs_sem)
     fetch.start()
     bar = pltpu.get_barrier_semaphore()
-    for i in range(ROW):
-        for j in range(CHAN):
-            if i or j:
-                peer = (base + lax.rem(spot + i, ROW), lax.rem(plane + j, CHAN))
-                pl.semaphore_signal(bar, inc=1, device_id=peer, device_id_type=MESH)
     pl.semaphore_signal(bar, inc=1, device_id=above, device_id_type=MESH)
     pl.semaphore_signal(bar, inc=1, device_id=below, device_id_type=MESH)
+    order = [(i, j) for j in (2, 1, 3, 0) for i in (4, 5, 2, 3, 6, 7, 1, 0) if i or j]
+    for i, j in order:
+        peer = (base + lax.rem(spot + i, ROW), lax.rem(plane + j, CHAN))
+        pl.semaphore_signal(bar, inc=1, device_id=peer, device_id_type=MESH)
     pl.semaphore_wait(bar, ROW * CHAN + 1)
 
     def send(src, t, h):
@@ -76,7 +75,7 @@
         pltpu.make_async_copy(src.at[:, columns(spot, plane)], dst, arrival).start()
 
         def one(n, carry):
-            room = lax.rem(spot + n // CHAN, ROW)
+            room = lax.rem(spot + 3 * lax.rem(n, ROW) + n // ROW, ROW)
             floor = lax.rem(plane + lax.rem(n, CHAN), CHAN)
             pltpu.make_async_remote_copy(
                 src_ref=src.at[:, columns(room, floor)],

time: 104 us -> 104 us (level)
  no operation moved by 1% of the time
where the time goes in v5:
time: 104 us; the launch traced here: 103 us
  Pallas kernels  103 us (99%)
    pallas_call x1, Pallas kernels, whole(): pl.pallas_call(functools.partial(whole_kernel, rows_total), out_shape=jax...  101 us

profile of v5, /device:TPU:1, one launch (start us, length us, event | category | flops | bytes accessed | tf_op | source)
XLA Modules:
  0.0 103.4 jit_solution(16030061735626853191)
XLA Ops:
  0.6 100.8 %whole_rows.1.land = bf16[4,2,8,256,128]{4,3,2,1,0:T(8,128)(2,1)S(1)} custom-call(bf16[64,8192]{1,0:T(8,128)(2,1)} %q.1, bf16[64,8192]{1,0:T(8,128)(2,1)} %k.1, bf16[64,8192]{1,0:T(8,128)(2,1)} %v.1, bf16[64,8192]{1,0:T(8,128)(2,1)} %g.1, s32[64,128]{1,0:T(8,128)} %bitcast.1), custom_call_target="tpu_custom_call" | custom-call | tf_op jit(solution)/shard_map/whole_rows/pallas_call | solution.py:287
  101.4 2.0 %lay_out.1 = (bf16[256,2048]{1,0:T(8,128)(2,1)}, bf16[256,2048]{1,0:T(8,128)(2,1)}, bf16[256,2048]{1,0:T(8,128)(2,1)}, bf16[256,2048]{1,0:T(8,128)(2,1)}) custom-call(bf16[4,2,8,256,128]{4,3,2,1,0:T(8,128)(2,1)S(1)} %whole_rows.1.land), custom_call_target="tpu_custom_call" | custom-call | tf_op jit(solution)/shard_map/lay_out/pallas_call | solution.py:337

commit v6 on v5

--- a/solution.py
+++ b/solution.py
@@ -139,10 +139,14 @@
     def rows_at(offset):
         return pl.ds(pl.multiple_of(offset, TOK), TOK)
 
-    def home_queries(h):
+    def home_queries(h, upper):
         for t in range(2):
             for i in range(ROW):
-                go_home(og.at[t, h, rows_at(lax.rem(spot + i, ROW) * TOK), :], t, h, i)
+                other = lax.rem(spot + i, ROW)
+
+                @pl.when((other >= 4) if upper else (other < 4))
+                def _():
+                    go_home(og.at[t, h, rows_at(other * TOK), :], t, h, i)
 
     def home_keys(h):
         for t in range(2):
@@ -254,10 +258,11 @@
     settle(0, 0, 4)
     for t in range(2):
         drop(t, 0).start()
+    home_queries(0, False)
     attend(0, 4, 8)
     raise_half(1, 1)
     settle(0, 4, 12)
-    home_queries(0)
+    home_queries(0, True)
     arrive(1)
     join(0)
     prepare(1)
@@ -265,9 +270,10 @@
     settle(1, 0, 4)
     for t in range(2):
         drop(t, 1).start()
+    home_queries(1, False)
     attend(1, 4, 8)
     settle(1, 4, 12)
-    home_queries(1)
+    home_queries(1, True)
     join(1)
 
     for h in range(2):

time: 104 us -> 103 us (level)
  no operation moved by 1% of the time
where the time goes in v6:
time: 103 us
  Pallas kernels  102 us (99%)
    pallas_call x1, Pallas kernels, whole(): pl.pallas_call(functools.partial(whole_kernel, rows_total), out_shape=jax...  100 us

profile of v6, /device:TPU:1, one launch (start us, length us, event | category | flops | bytes accessed | tf_op | source)
XLA Modules:
  0.0 103.1 jit_solution(8824471572035342259)
XLA Ops:
  0.6 100.5 %whole_rows.1.land = bf16[4,2,8,256,128]{4,3,2,1,0:T(8,128)(2,1)S(1)} custom-call(bf16[64,8192]{1,0:T(8,128)(2,1)} %q.1, bf16[64,8192]{1,0:T(8,128)(2,1)} %k.1, bf16[64,8192]{1,0:T(8,128)(2,1)} %v.1, bf16[64,8192]{1,0:T(8,128)(2,1)} %g.1, s32[64,128]{1,0:T(8,128)} %bitcast.1), custom_call_target="tpu_custom_call" | custom-call | tf_op jit(solution)/shard_map/whole_rows/pallas_call | solution.py:293
  101.1 2.0 %lay_out.1 = (bf16[256,2048]{1,0:T(8,128)(2,1)}, bf16[256,2048]{1,0:T(8,128)(2,1)}, bf16[256,2048]{1,0:T(8,128)(2,1)}, bf16[256,2048]{1,0:T(8,128)(2,1)}) custom-call(bf16[4,2,8,256,128]{4,3,2,1,0:T(8,128)(2,1)S(1)} %whole_rows.1.land), custom_call_target="tpu_custom_call" | custom-call | tf_op jit(solution)/shard_map/lay_out/pallas_call | solution.py:343
